TPU v7x, 128 devices: a whole 4x4x4 slice. The times are simulated.
128 devices in a mesh: rep: 4 (over z_lo, core), row: 8 (over z_hi, y), col: 4 (over x).
Axes of the slice: x: 4, y: 4, z: 4 (z_hi: 2, z_lo: 2; z = z_hi * 2 + z_lo), core: 2. Of those that a mesh axis runs over, the one named last changes fastest.
Arguments:
- activations: bfloat16 [4096, 8192], P(('rep', 'row'), 'col'), may hold values from -12 to 12
- target: bfloat16 [4096, 8192], P(('rep', 'col'), 'row'), may hold values from -6 to 6
- weight: bfloat16 [8192, 8192], P('col', 'row'), may hold values from -0.0625 to 0.0625
- probe_codes: int32 [4, 8], P('col', 'row'), may hold values from 0 to 1073741823
Outputs:
- step: bfloat16 [8192, 8192], P('col', 'row')
All inputs are finite; a program needn't handle non-finite values.
Results may differ from a plain program's by a relative error of at most 0.018.
Values may be sent and summed in bfloat16 or wider, within the bound.
A program may use at most 128 MiB of HBM per device.

v0:
```python
import math

import jax
import jax.numpy as jnp
from jax import lax
from jax.sharding import PartitionSpec as P

AVG = 128


def sent_to_all(x, axis):
    copies = jnp.broadcast_to(x, (lax.axis_size(axis), *x.shape))
    return lax.all_to_all(copies, axis, split_axis=0, concat_axis=0, tiled=True)


def of_everyone(x, axis):
    everything = sent_to_all(x, axis)
    return jnp.sum(everything.astype(jnp.float32), axis=0)


def probe_signs(tile_code, local_rows, local_cols):
    mixed = local_rows * 1664525 + local_cols * 22695477 + tile_code * 1013904223
    mixed = mixed ^ mixed >> 15 & 131071
    mixed = mixed * 1274126177
    mixed = mixed ^ mixed >> 13 & 524287
    parity = mixed >> 7 & 1
    return (1 - 2 * parity).astype(jnp.float32).astype(jnp.bfloat16)


def block_means(curvature):
    rows, cols = curvature.shape
    return curvature.reshape(rows, cols // AVG, AVG).mean(axis=2)


def finish(gradient, blockmean):
    rows, cols = gradient.shape
    denom = jnp.maximum(jnp.abs(blockmean), 0.25)[:, :, None]
    update = gradient.reshape(rows, cols // AVG, AVG) / denom
    return update.reshape(rows, cols).astype(jnp.bfloat16)


def contract(left, right):
    return lax.dot_general(
        left, right, (((0,), (0,)), ((), ())), preferred_element_type=jnp.float32
    )


def shards(activations, target, weight, probe_codes):
    rows_tile, cols_tile = weight.shape
    local_rows = jnp.arange(rows_tile, dtype=jnp.int32)[:, None]
    local_cols = jnp.arange(cols_tile, dtype=jnp.int32)[None, :]
    probe = probe_signs(probe_codes[0, 0], local_rows, local_cols)
    operands = jnp.concatenate([weight, probe], axis=1)
    share = target.shape[0]
    tokens_micro = share * lax.axis_size("col")
    total = tokens_micro * lax.axis_size("rep")
    gathered = lax.all_gather(activations, "row", axis=0, tiled=True)
    sums = lax.psum_scatter(
        jnp.dot(gathered, operands, preferred_element_type=jnp.float32).astype(jnp.bfloat16),
        "col",
        scatter_dimension=0,
        tiled=True,
    ).astype(jnp.float32)
    error = (sums[:, :cols_tile] - target.astype(jnp.float32)).astype(jnp.bfloat16)
    tangent = sums[:, cols_tile:].astype(jnp.bfloat16)
    packed = jnp.concatenate([error, tangent], axis=1)
    all_rows = lax.all_gather(packed, "col", axis=0, tiled=True)
    contracted = contract(gathered, all_rows)
    grad_part = (contracted[:, :cols_tile] * (1.0 / math.sqrt(total))).astype(jnp.bfloat16)
    curv_part = probe.astype(jnp.float32) * contracted[:, cols_tile:] * (1.0 / total)
    blockmean = of_everyone(block_means(curv_part).astype(jnp.bfloat16), "rep").astype(jnp.float32)
    gradient = lax.psum_scatter(grad_part, "rep", scatter_dimension=0, tiled=True).astype(
        jnp.float32
    )
    own_rows = gradient.shape[0]
    own_means = lax.dynamic_slice_in_dim(blockmean, lax.axis_index("rep") * own_rows, own_rows, 0)
    piece_step = finish(gradient, own_means)
    return lax.all_gather(piece_step, "rep", axis=0, tiled=True)


def solution(mesh):
    placed = (P(("rep", "row"), "col"), P(("rep", "col"), "row"), P("col", "row"), P("col", "row"))
    return jax.shard_map(
        shards, mesh=mesh, in_specs=placed, out_specs=P("col", "row"), check_vma=False
    )
```

profile of v0, /device:TPU:1, one launch (start us, length us, event | category | flops | bytes accessed | tf_op | source)
XLA Modules:
  0.0 330.8 jit_solution(2561261139024598522)
XLA Ops:
  6.5 0.0 all-gather.4.cloned.1.call-start
  6.5 0.7 all-gather.4.cloned.1.call-update
  7.3 0.0 reduce-scatter.3.cloned.1.call-start
  7.9 6.5 %copy.8 = bf16[2048,1024]{0,1:T(8,128)(2,1)} copy(bf16[2048,1024]{1,0:T(8,128)(2,1)} %param.6) | data formatting | bytes 8388608 | tf_op args[2]
  14.5 5.4 %convert_convert_fusion = bf16[2048,1024]{0,1:T(8,128)(2,1)} fusion(s32[]{:T(128)} %bitcast, s32[1024]{0:T(1024)S(1)} %iota_multiply_fusion.1, s32[2048]{0:T(1024)S(1)} %iota_multiply_fusion), kind=kLoop, calls=%fused_computation.10 | loop fusion | flops 31457280 | bytes 4206596 | tf_op jit(solution)/shard_map/convert_element_type | solution.py:27
  19.9 64.0 %all-gather.4.cloned.1.call-done = bf16[1024,2048]{1,0:T(8,128)(2,1)} async-done(((bf16[128,2048]{1,0:T(8,128)(2,1)}), bf16[1024,2048]{1,0:T(8,128)(2,1)}) %all-gather.4.cloned.1.call-update) | async-done | bytes 4194320 | tf_op jit(solution)/shard_map/all_gather | solution.py:57
  83.9 14.5 %convert_bitcast_fusion = bf16[1024,2048]{0,1:T(8,128)(2,1)} fusion(bf16[1024,2048]{1,0:T(8,128)(2,1)} %all-gather.4.cloned.1.call-done, bf16[2048,1024]{0,1:T(8,128)(2,1)} %convert_convert_fusion, bf16[2048,1024]{0,1:T(8,128)(2,1)} %copy.8), kind=kOutput, calls=%fused_computation.11 | convolution fusion | flops 8608808960 | bytes 16777216 | tf_op jit(solution)/shard_map/dot_general | solution.py:59
  98.4 0.0 reduce-scatter.3.cloned.1.call-update
  98.4 0.0 all-gather.6.cloned.1.call-start
  98.5 0.0 copy-done.1
  98.5 0.2 copy.9
  98.7 45.0 %reduce-scatter.3.cloned.1.call-done = bf16[256,2048]{0,1:T(8,128)(2,1)} async-done(((bf16[1024,2048]{0,1:T(8,128)(2,1)}), bf16[256,2048]{0,1:T(8,128)(2,1)}) %reduce-scatter.3.cloned.1.call-update) | async-done | bytes 1048592 | tf_op jit(solution)/shard_map/reduce_scatter | solution.py:58
  143.7 1.1 slice.22
  144.8 1.2 subtract_convert_fusion
  146.0 1.0 pad_maximum_fusion
  147.0 0.0 all-gather.6.cloned.1.call-update
  147.0 0.2 reduce-scatter.5.cloned.1.call-start
  147.3 49.7 %all-gather.6.cloned.1.call-done = bf16[1024,2048]{0,1:T(8,128)(2,1)} async-done(((bf16[256,2048]{0,1:T(8,128)(2,1)}), bf16[1024,2048]{0,1:T(8,128)(2,1)}) %all-gather.6.cloned.1.call-update) | async-done | bytes 4194320 | tf_op jit(solution)/shard_map/all_gather | solution.py:67
  197.0 12.1 %convolution_bitcast_fusion = f32[2048,2048]{0,1:T(8,128)S(1)} fusion(bf16[1024,2048]{0,1:T(8,128)(2,1)} %all-gather.6.cloned.1.call-done, bf16[1024,2048]{1,0:T(8,128)(2,1)} %all-gather.4.cloned.1.call-done), kind=kOutput, calls=%fused_computation | convolution fusion | flops 8589934592 | bytes 25165824 | tf_op jit(solution)/shard_map/dot_general | solution.py:43
  209.1 0.0 copy-start
  209.1 5.7 %copy-done = f32[2048,2048]{0,1:T(8,128)} copy-done((f32[2048,2048]{0,1:T(8,128)}, f32[2048,2048]{0,1:T(8,128)S(1)}, u32[]{:S(2)}) %copy-start) | copy-done | bytes 16777240
  214.8 3.2 fusion.1
  218.1 0.0 reduce-scatter.5.cloned.1.call-update
  218.1 6.7 %bitcast_reduce_fusion = f32[2048,8]{0,1:T(8,128)S(1)} fusion(f32[2048,2048]{0,1:T(8,128)} %copy-done, s32[]{:T(128)} %bitcast, s32[1024]{0:T(1024)S(1)} %iota_multiply_fusion.1, s32[2048]{0:T(1024)S(1)} %iota_multiply_fusion), kind=kLoop, calls=%fused_computation.9 | loop fusion | flops 39829504 | bytes 8466436 | tf_op jit(solution)/shard_map/reduce_sum | solution.py:32
  224.8 0.7 broadcast_in_dim.2
  225.5 5.3 %all-to-all-start = ((bf16[4,2048,8]{1,2,0:T(8,128)(2,1)}), bf16[4,2048,8]{1,2,0:T(8,128)(2,1)S(1)}, u32[]{:S(2)}, u32[]{:S(2)}) async-start(bf16[4,2048,8]{1,2,0:T(8,128)(2,1)} %broadcast_in_dim.2), calls=%async_computation.2 | async-start | bytes 262144 | tf_op jit(solution)/shard_map/all_to_all | solution.py:13
  230.8 5.7 %all-to-all-done = bf16[4,2048,8]{1,2,0:T(8,128)(2,1)S(1)} async-done(((bf16[4,2048,8]{1,2,0:T(8,128)(2,1)}), bf16[4,2048,8]{1,2,0:T(8,128)(2,1)S(1)}, u32[]{:S(2)}, u32[]{:S(2)}) %all-to-all-start) | async-done | bytes 131104 | tf_op jit(solution)/shard_map/all_to_all | solution.py:13
  236.6 31.0 %reduce-scatter.5.cloned.1.call-done = bf16[512,1024]{0,1:T(8,128)(2,1)} async-done(((bf16[2048,1024]{0,1:T(8,128)(2,1)}), bf16[512,1024]{0,1:T(8,128)(2,1)}) %reduce-scatter.5.cloned.1.call-update) | async-done | bytes 1048592 | tf_op jit(solution)/shard_map/reduce_scatter | solution.py:72
  267.6 2.4 fusion.8
  270.0 0.0 all-gather.8.cloned.1.call-update
  270.0 47.8 %all-gather.8.cloned.1.call-done = bf16[2048,1024]{0,1:T(8,128)(2,1)} async-done(((bf16[512,1024]{0,1:T(8,128)(2,1)}), bf16[2048,1024]{0,1:T(8,128)(2,1)}) %all-gather.8.cloned.1.call-update) | async-done | bytes 4194320 | tf_op jit(solution)/shard_map/all_gather | solution.py:78
  317.8 6.4 %copy.10 = bf16[2048,1024]{1,0:T(8,128)(2,1)} copy(bf16[2048,1024]{0,1:T(8,128)(2,1)} %all-gather.8.cloned.1.call-done) | data formatting | bytes 8388608 | tf_op jit(solution)/shard_map/all_gather | solution.py:78
  (7 shorter events, 0.1 us)
Async XLA Ops:
  6.5 77.3 %all-gather.4.cloned.1.call-start = ((), (), s32[]{:S(2)}) async-start(), calls=%async_computation.3 | async-start | bytes 4718592 | tf_op jit(solution)/shard_map/all_gather | solution.py:57
  7.3 136.5 %reduce-scatter.3.cloned.1.call-start = ((), (), s32[]{:S(2)}) async-start(), calls=%async_computation.4 | async-start | bytes 5242880 | tf_op jit(solution)/shard_map/reduce_scatter | solution.py:58
  19.9 78.6 %copy-start.1 = (bf16[256,1024]{1,0:T(8,128)(2,1)S(1)}, bf16[256,1024]{1,0:T(8,128)(2,1)}, u32[]{:S(2)}) copy-start(bf16[256,1024]{1,0:T(8,128)(2,1)} %param.5) | copy-start | bytes 1572868
  98.4 98.5 %all-gather.6.cloned.1.call-start = ((), (), s32[]{:S(2)}) async-start(), calls=%async_computation.5 | async-start | bytes 5242880 | tf_op jit(solution)/shard_map/all_gather | solution.py:67
  147.0 120.6 %reduce-scatter.5.cloned.1.call-start = ((), (), s32[]{:S(2)}) async-start(), calls=%async_computation.6 | async-start | bytes 5242880 | tf_op jit(solution)/shard_map/reduce_scatter | solution.py:72
  209.1 5.7 %copy-start = (f32[2048,2048]{0,1:T(8,128)}, f32[2048,2048]{0,1:T(8,128)S(1)}, u32[]{:S(2)}) copy-start(f32[2048,2048]{0,1:T(8,128)S(1)} %convolution_bitcast_fusion) | copy-start | bytes 50331652
  225.5 11.0 %all-to-all-start = ((bf16[4,2048,8]{1,2,0:T(8,128)(2,1)}), bf16[4,2048,8]{1,2,0:T(8,128)(2,1)S(1)}, u32[]{:S(2)}, u32[]{:S(2)}) async-start(bf16[4,2048,8]{1,2,0:T(8,128)(2,1)} %broadcast_in_dim.2), calls=%async_computation.2 | async-start | bytes 262144 | tf_op jit(solution)/shard_map/all_to_all | solution.py:13
  230.8 87.0 %all-gather.8.cloned.1.call-start = ((), (), s32[]{:S(2)}) async-start(), calls=%async_computation.7 | async-start | bytes 5242880 | tf_op jit(solution)/shard_map/all_gather | solution.py:78
Sparse Core Ops, SparseCore 0:
  9.7 74.1 all-gather.3
  98.5 45.1 reduce-scatter.2
  147.2 49.7 all-gather.5
  218.2 49.3 reduce-scatter.4
  270.1 47.6 all-gather.7
where the time goes:
time: 331 us
  waiting for transfers between devices  244 us (74%)
  matrix products  26.7 us (8%)
  local copies, waits for them, and re-layouts  20.6 us (6%)
  other arithmetic  20 us (6%)
  between operations  13.8 us (4%)
  starting transfers between devices  5.64 us (2%)
    all_gather x1, waiting for transfers between devices, shards(): gathered = lax.all_gather(activations, 'row', axis=0, tiled=True)  64 us
    all_gather x1, waiting for transfers between devices, shards(): all_rows = lax.all_gather(packed, 'col', axis=0, tiled=True)  49.7 us
    all_gather x1, waiting for transfers between devices, shards(): return lax.all_gather(piece_step, 'rep', axis=0, tiled=True)  47.8 us
    reduce_scatter x1, waiting for transfers between devices, shards(): lax.psum_scatter(jnp.dot(gathered, operands, preferred_element_type=jnp.f...  45 us
    reduce_scatter x1, waiting for transfers between devices, shards(): lax.psum_scatter(grad_part, 'rep', scatter_dimension=0, tiled=True)  31 us
    dot_general x1, matrix products, shards(): jnp.dot(gathered, operands, preferred_element_type=jnp.float32)  14.5 us
    unnamed x6, local copies, waits for them, and re-layouts  12.5 us
    dot_general x1, matrix products, contract(): lax.dot_general(left, right, (((0,), (0,)), ((), ())), preferred_element_...  12.1 us
  transfers between devices with their start and end apart: 6, of which 6 were waited for; matrix products, arithmetic and copies ran while one was open for 6% of the time, Pallas kernels for 0%

commit v1 on v0

v1 whole, which is shorter than its diff:
```python
import functools
import math

import jax
import jax.numpy as jnp
from jax import lax
from jax.experimental import pallas as pl
from jax.experimental.pallas import tpu as pltpu
from jax.sharding import PartitionSpec as P

MESH = pl.DeviceIdType.MESH
BF = jnp.bfloat16
F32 = jnp.float32
AVG = 128
SUB = 16
GROUPS = ((0, 1, None), (1, 4, 0), (1, 4, 1), (4, 5, None), (5, 8, 0), (5, 8, 1))


def wrapped(value):
    return (value + 2**31) % 2**32 - 2**31


def remote(src, dst, send, recv, peer):
    return pltpu.make_async_remote_copy(
        src_ref=src, dst_ref=dst, send_sem=send, recv_sem=recv,
        device_id=peer, device_id_type=MESH,
    )


def kernel(
    grad_scale, curv_scale, code_ref, x_hbm, y_hbm, w_hbm, out_hbm,
    xg, w, y, pt, own, hold_e, hold_t, sb_p, sb_m, s2_p, s2_m, rb_p, rb_m, r2_p, r2_m,
    et, g_own, m_own, g_send, m_send, g_recv, m_recv, h_send, n_send, h_recv, n_recv, stage,
    load_sem, xs, xr, rs_s, rs_r, ag_s, ag_r, co_s, co_r, zs, zr, fs, fr, ls,
):
    rep, row, col = lax.axis_index("rep"), lax.axis_index("row"), lax.axis_index("col")
    plane, ypos = row // 4, row % 4
    core = rep % 2
    right, left, far = (col + 1) % 4, (col + 3) % 4, (col + 2) % 4
    to_right, to_left = {"col": right}, {"col": left}
    up, down = {"row": plane * 4 + (ypos + 1) % 4}, {"row": plane * 4 + (ypos + 3) % 4}
    across = {"row": (row + 4) % 8}
    twin = {"rep": rep - core + (1 - core)}
    zmate = {"rep": (rep + 2) % 4}
    rows, cols = w.shape
    nc = cols // AVG
    half = rows // 2

    loads = [
        pltpu.make_async_copy(x_hbm, xg.at[:, 0], load_sem.at[0]),
        pltpu.make_async_copy(w_hbm, w, load_sem.at[1]),
        pltpu.make_async_copy(y_hbm, y, load_sem.at[2]),
    ]
    for load in loads:
        load.start()

    barrier = pltpu.get_barrier_semaphore()
    peers = (to_right, to_left, up, down, across, twin, zmate)
    for peer in peers:
        pl.semaphore_signal(barrier, inc=1, device_id=peer, device_id_type=MESH)
    pl.semaphore_wait(barrier, len(peers))
    loads[0].wait()

    sent = []

    def pass_on(slot, part, peer, landing):
        k = len(sent)
        copy = remote(xg.at[:, slot, part], xg.at[:, landing, part], xs.at[k], xr.at[landing, part], peer)
        copy.start()
        sent.append(copy)

    def arrived(slot, part):
        remote(xg.at[:, slot, part], xg.at[:, slot, part], xs.at[0], xr.at[slot, part], across).wait_recv()

    for part in range(2):
        pass_on(0, part, across, 1)
        pass_on(0, part, up, 3)
        pass_on(0, part, down, 2)

    loads[1].wait()
    loads[2].wait()

    slot_rows = []
    other = 1 - plane
    for pl_, dy in ((plane, 0), (other, 0), (plane, 1), (plane, 3), (plane, 2), (other, 1), (other, 3), (other, 2)):
        slot_rows.append(pl_ * 4 + (ypos + dy) % 4)

    def units(group):
        lo, hi, part = GROUPS[group]
        return [(s, h) for s in range(lo, hi) for h in ((0, 1) if part is None else (part,))]

    def view(ref, group, lanes=slice(None)):
        lo, hi, part = GROUPS[group]
        return ref.at[lo:hi, :, :, lanes] if part is None else ref.at[lo:hi, part, :, lanes]

    def members(group):
        lo, hi, part = GROUPS[group]
        n = len(units(group))
        pieces = []
        for k in range(4):
            dest = (col + k) % 4
            piece = xg[dest, lo:hi] if part is None else xg[dest, lo:hi, part]
            pieces.append(piece.reshape(n * SUB, rows))
        return jnp.concatenate(pieces, axis=0)

    def put(ref, group, lanes, value):
        lo, hi, part = GROUPS[group]
        if part is None:
            ref[lo:hi, :, :, lanes] = value.reshape(hi - lo, 2, SUB, value.shape[-1])
        else:
            ref[lo:hi, part, :, lanes] = value.reshape(hi - lo, SUB, value.shape[-1])

    def get(ref, group, lanes):
        lo, hi, part = GROUPS[group]
        value = ref[lo:hi, :, :, lanes] if part is None else ref[lo:hi, part, :, lanes]
        return value.reshape(len(units(group)) * SUB, value.shape[-1])

    BLOCK = 256

    def errors(group):
        n = len(units(group)) * SUB

        def step(j, carry):
            lanes = pl.ds(pl.multiple_of(j * BLOCK, BLOCK), BLOCK)
            sums = jnp.dot(members(group), w[:, lanes], preferred_element_type=F32)
            parts = []
            for k in range(4):
                dest = (col + k) % 4
                wanted = []
                for s, h in units(group):
                    mine = (slot_rows[s] // 2 == col).astype(F32)
                    wanted.append(y[slot_rows[s] % 2, dest, h, :, lanes].astype(F32) * mine)
                parts.append(sums[k * n:(k + 1) * n] - jnp.concatenate(wanted, axis=0))
            put(own, group, lanes, parts[0])
            put(hold_e, group, lanes, parts[1])
            put(sb_p, group, lanes, parts[2].astype(BF))
            put(sb_m, group, lanes, parts[3].astype(BF))
            return carry

        lax.fori_loop(0, cols // BLOCK, step, 0)

    def tangents(group):
        n = len(units(group)) * SUB

        def step(j, carry):
            start = pl.multiple_of(j * BLOCK, BLOCK)
            lanes, shifted = pl.ds(start, BLOCK), pl.ds(pl.multiple_of(cols + start, BLOCK), BLOCK)
            sums = lax.dot_general(
                members(group), pt[lanes, :], (((1,), (1,)), ((), ())), preferred_element_type=F32
            )
            parts = [sums[k * n:(k + 1) * n] for k in range(4)]
            put(own, group, shifted, parts[0])
            put(sb_p, group, shifted, parts[1].astype(BF))
            put(sb_m, group, shifted, parts[2].astype(BF))
            put(hold_t, group, lanes, parts[3])
            return carry

        lax.fori_loop(0, cols // BLOCK, step, 0)

    def first_hop(group):
        return [
            remote(view(sb_p, group), view(rb_p, group), rs_s.at[0, group], rs_r.at[0, group], to_right),
            remote(view(sb_m, group), view(rb_m, group), rs_s.at[1, group], rs_r.at[1, group], to_left),
        ]

    def second_hop(group):
        return [
            remote(view(s2_p, group), view(r2_p, group), rs_s.at[2, group], rs_r.at[2, group], to_right),
            remote(view(s2_m, group), view(r2_m, group), rs_s.at[3, group], rs_r.at[3, group], to_left),
        ]

    def relay(group):
        for copy in first_hop(group):
            copy.wait_recv()
        low, high = slice(0, cols), slice(cols, 2 * cols)
        put(s2_p, group, low, (get(hold_e, group, low) + get(rb_p, group, low).astype(F32)).astype(BF))
        put(s2_m, group, low, (get(hold_t, group, low) + get(rb_m, group, high).astype(F32)).astype(BF))
        for copy in second_hop(group):
            copy.start()

    def probe_signs():
        code = code_ref[0, 0] * 1013904223
        lane = lax.broadcasted_iota(jnp.int32, (SUB, 512), 1) * 1664525
        sub = lax.broadcasted_iota(jnp.int32, (SUB, 512), 0) * 22695477
        base = lane + sub + code

        def step(j, carry):
            for i in range(rows // 512):
                mixed = base + (j * (SUB * 22695477) + wrapped(i * 512 * 1664525))
                mixed = mixed ^ mixed >> 15 & 131071
                mixed = mixed * 1274126177
                mixed = mixed ^ mixed >> 13 & 524287
                parity = mixed >> 7 & 1
                pt[pl.ds(pl.multiple_of(j * SUB, SUB), SUB), i * 512:(i + 1) * 512] = (
                    (1 - 2 * parity).astype(F32).astype(BF)
                )
            return carry

        lax.fori_loop(0, cols // SUB, step, 0)

    errors(0)
    probe_signs()
    tangents(0)
    for copy in first_hop(0):
        copy.start()

    def forward_first():
        for s in (1, 2, 3):
            arrived(s, 0)
        pass_on(3, 0, up, 4)
        pass_on(1, 0, up, 6)
        pass_on(1, 0, down, 5)

    def forward_second():
        for s in (1, 2, 3):
            arrived(s, 1)
        pass_on(2, 1, down, 4)
        pass_on(1, 1, up, 6)
        pass_on(1, 1, down, 5)

    def forward_third():
        for part in range(2):
            arrived(4, part)
            pass_on(4, part, across, 7)

    def last(part):
        for s in (5, 6, 7):
            arrived(s, part)

    ready = (None, forward_first, forward_second, forward_third, lambda: last(0), lambda: last(1))
    for group in range(1, len(GROUPS)):
        ready[group]()
        errors(group)
        tangents(group)
        for copy in first_hop(group):
            copy.start()
        relay(group - 1)
    relay(len(GROUPS) - 1)
    for group in range(len(GROUPS)):
        for copy in second_hop(group):
            copy.wait_recv()

    def own_block(c):
        return [
            remote(et.at[c, col], et.at[c, col], ag_s.at[0, c], ag_r.at[0, c], to_right),
            remote(et.at[c, col], et.at[c, col], ag_s.at[1, c], ag_r.at[1, c], to_left),
        ]

    def far_block(c):
        first, second = slice(0, AVG), slice(AVG, 2 * AVG)
        return [
            remote(et.at[c, left, first], et.at[c, left, first], ag_s.at[2, c], ag_r.at[2, c], to_right),
            remote(et.at[c, right, second], et.at[c, right, second], ag_s.at[3, c], ag_r.at[3, c], to_left),
        ]

    def twin_block(c):
        return [
            remote(g_send.at[c], g_recv.at[c], co_s.at[0, c], co_r.at[0, c], twin),
            remote(m_send.at[c], m_recv.at[c], co_s.at[1, c], co_r.at[1, c], twin),
        ]

    def z_block(c):
        return [
            remote(h_send.at[c], h_recv.at[c], zs.at[0, c], zr.at[0, c], zmate),
            remote(n_send.at[c], n_recv.at[c], zs.at[1, c], zr.at[1, c], zmate),
        ]

    def result(c):
        area = out_hbm.at[
            pl.ds(pl.multiple_of(core * half, half), half), pl.ds(pl.multiple_of(c * AVG, AVG), AVG)
        ]
        return remote(stage.at[c], area, fs.at[c], fr.at[c], twin), pltpu.make_async_copy(
            stage.at[c], area, ls.at[c]
        )

    tokens = own.shape[0] * own.shape[1] * SUB

    def share(c):
        low = pl.ds(pl.multiple_of(c * AVG, AVG), AVG)
        high = pl.ds(pl.multiple_of(cols + c * AVG, AVG), AVG)

        def all_of(ref, lanes):
            return ref[:, :, :, lanes].reshape(tokens, AVG).astype(F32)

        error = all_of(own, low) + all_of(rb_m, low) + all_of(r2_p, low)
        tangent = all_of(own, high) + all_of(rb_p, high) + all_of(r2_m, low)
        et[c, col, 0:AVG] = error.T.astype(BF)
        et[c, col, AVG:2 * AVG] = tangent.T.astype(BF)
        for copy in own_block(c):
            copy.start()

    def far_share(c):
        for copy in own_block(c):
            copy.wait_recv()
        for copy in far_block(c):
            copy.start()

    PART = 512

    def contract(c):
        for copy in far_block(c):
            copy.wait_recv()
        both = jnp.concatenate([et[c, k] for k in range(4)], axis=1)
        signs = pl.ds(pl.multiple_of(c * AVG, AVG), AVG)

        def piece(owner, p):
            start = pl.multiple_of(owner * half + p * PART, PART)
            x = xg[:, :, :, :, pl.ds(start, PART)].reshape(4 * tokens, PART)
            sums = jnp.dot(both, x, preferred_element_type=F32)
            curv = sums[AVG:] * pt[signs, pl.ds(start, PART)].astype(F32)
            return sums[:AVG] * grad_scale, jnp.sum(curv, axis=0, keepdims=True) * curv_scale

        def put_means(ref, p, means):
            for k in range(PART // 128):
                ref[p * (PART // 128) + k:p * (PART // 128) + k + 1, :] = means[:, k * 128:(k + 1) * 128]

        for p in range(half // PART):
            gradient, means = piece(1 - core, p)
            g_send[c, :, p * PART:(p + 1) * PART] = gradient.astype(BF)
            put_means(m_send.at[c], p, means)
        for copy in twin_block(c):
            copy.start()
        for p in range(half // PART):
            gradient, means = piece(core, p)
            g_own[c % 2, :, p * PART:(p + 1) * PART] = gradient
            put_means(m_own.at[c % 2], p, means)

    def reduce_twin(c):
        for copy in twin_block(c):
            copy.wait_recv()
        h_send[c] = (g_own[c % 2] + g_recv[c].astype(F32)).astype(BF)
        n_send[c] = m_own[c % 2] + m_recv[c]
        for copy in z_block(c):
            copy.start()

    def divide(c):
        for copy in z_block(c):
            copy.wait_recv()
        means = n_send[c] + n_recv[c]
        denom = jnp.maximum(jnp.abs(means), 0.25)
        for k in range(half // 128):
            lanes = slice(k * 128, (k + 1) * 128)
            gradient = h_send[c, :, lanes].astype(F32) + h_recv[c, :, lanes].astype(F32)
            stage[c, lanes, :] = (gradient / denom[k:k + 1, :]).T.astype(BF)
        for copy in result(c):
            copy.start()

    LAG = 7

    def main(t, carry):
        @pl.when(t < nc)
        def _():
            share(t)

        @pl.when((t >= 1) & (t < nc + 1))
        def _():
            far_share(t - 1)

        @pl.when((t >= 2) & (t < nc + 2))
        def _():
            contract(t - 2)

        @pl.when((t >= 3) & (t < nc + 3))
        def _():
            reduce_twin(t - 3)

        @pl.when(t >= LAG)
        def _():
            divide(t - LAG)

        return carry

    lax.fori_loop(0, nc + LAG, main, 0)

    for copy in sent:
        copy.wait_send()
    for group in range(len(GROUPS)):
        for copy in first_hop(group) + second_hop(group):
            copy.wait_send()

    def drain(c, carry):
        for copy in own_block(c) + far_block(c) + twin_block(c) + z_block(c):
            copy.wait_send()
        there, here = result(c)
        there.wait()
        here.wait()
        return carry

    lax.fori_loop(0, nc, drain, 0)


def shards(activations, target, weight, probe_codes):
    share, rows = activations.shape
    cols = weight.shape[1]
    nc = cols // AVG
    tokens_micro = share * lax.axis_size("row")
    total = tokens_micro * lax.axis_size("rep")
    x = activations.reshape(4, 2, SUB, rows)
    y = target.reshape(2, 4, 2, SUB, cols)
    half = rows // 2
    vmem = pltpu.VMEM
    dma = pltpu.SemaphoreType.DMA
    return pl.pallas_call(
        functools.partial(kernel, 1.0 / math.sqrt(total), 1.0 / total / AVG),
        out_shape=jax.ShapeDtypeStruct((rows, cols), BF),
        in_specs=[pl.BlockSpec(memory_space=pltpu.SMEM)] + [pl.BlockSpec(memory_space=pl.ANY)] * 3,
        out_specs=pl.BlockSpec(memory_space=pl.ANY),
        scratch_shapes=[
            vmem((4, 8, 2, SUB, rows), BF),
            vmem((rows, cols), BF),
            vmem((2, 4, 2, SUB, cols), BF),
            vmem((cols, rows), BF),
            vmem((8, 2, SUB, 2 * cols), F32),
            vmem((8, 2, SUB, cols), F32),
            vmem((8, 2, SUB, cols), F32),
            vmem((8, 2, SUB, 2 * cols), BF),
            vmem((8, 2, SUB, 2 * cols), BF),
            vmem((8, 2, SUB, cols), BF),
            vmem((8, 2, SUB, cols), BF),
            vmem((8, 2, SUB, 2 * cols), BF),
            vmem((8, 2, SUB, 2 * cols), BF),
            vmem((8, 2, SUB, cols), BF),
            vmem((8, 2, SUB, cols), BF),
            vmem((nc, 4, 2 * AVG, 256), BF),
            vmem((2, AVG, half), F32),
            vmem((2, 8, 128), F32),
            vmem((nc, AVG, half), BF),
            vmem((nc, 8, 128), F32),
            vmem((nc, AVG, half), BF),
            vmem((nc, 8, 128), F32),
            vmem((nc, AVG, half), BF),
            vmem((nc, 8, 128), F32),
            vmem((nc, AVG, half), BF),
            vmem((nc, 8, 128), F32),
            vmem((nc, half, AVG), BF),
            dma((3,)),
            dma((14,)),
            dma((8, 2)),
            dma((4, 6)),
            dma((4, 6)),
            dma((4, nc)),
            dma((4, nc)),
            dma((2, nc)),
            dma((2, nc)),
            dma((2, nc)),
            dma((2, nc)),
            dma((nc,)),
            dma((nc,)),
            dma((nc,)),
        ],
        compiler_params=pltpu.CompilerParams(
            collective_id=0, has_side_effects=True, vmem_limit_bytes=62 * 1024 * 1024
        ),
    )(probe_codes, x, y, weight)


def solution(mesh):
    placed = (P(("rep", "row"), "col"), P(("rep", "col"), "row"), P("col", "row"), P("col", "row"))
    return jax.shard_map(
        shards, mesh=mesh, in_specs=placed, out_specs=P("col", "row"), check_vma=False
    )
```

time: 331 us -> 127 us (0.38)
  waiting for transfers between devices: 244 us -> 0 us
  Pallas kernels: 0 us -> 121 us
  matrix products: 26.7 us -> 0 us
  other arithmetic: 20 us -> 0 us
  local copies, waits for them, and re-layouts: 20.6 us -> 4.64 us
  between operations: 13.8 us -> 0.66 us
  starting transfers between devices: 5.64 us -> 0 us
    all_gather x3 -> x0, waiting for transfers between devices: 162 us -> none  [the longest x1 64 us: shards(): gathered = lax.all_gather(activations, 'row', axis=0, tiled=True)]
    pallas_call x0 -> x1, Pallas kernels: none -> 121 us  [shards(): pl.pallas_call(functools.partial(kernel, 1.0 / math.sqrt(total), 1.0 / to...]
    reduce_scatter x2 -> x0, waiting for transfers between devices: 76 us -> none  [the longest x1 45 us: shards(): lax.psum_scatter(jnp.dot(gathered, operands, preferred_element_type=jnp.f...]
    dot_general x2 -> x0, matrix products: 26.7 us -> none  [the longest x1 14.5 us: shards(): jnp.dot(gathered, operands, preferred_element_type=jnp.float32)]
    convert_element_type x5 -> x0, other arithmetic: 12.2 us -> none  [the longest x1 5.37 us: probe_signs(): return (1 - 2 * parity).astype(jnp.float32).astype(jnp.bfloat16)]
    unnamed x6 -> x1, local copies, waits for them, and re-layouts: 12.5 us -> 4.64 us
    reduce_sum x2 -> x0, other arithmetic: 6.75 us -> none  [the longest x1 6.73 us: block_means(): return curvature.reshape(rows, cols // AVG, AVG).mean(axis=2)]
    all_gather x1 -> x0, local copies, waits for them, and re-layouts: 6.39 us -> none  [shards(): return lax.all_gather(piece_step, 'rep', axis=0, tiled=True)]
  transfers between devices with their start and end apart: 6 -> 0, of which waited for: 6 -> 0; matrix products, arithmetic and copies ran while one was open for 6% -> 0% of each run, Pallas kernels for 0% -> 0%
where the time goes in v1:
time: 127 us
  Pallas kernels  121 us (95%)
  local copies, waits for them, and re-layouts  4.64 us (4%)
    pallas_call x1, Pallas kernels, shards(): pl.pallas_call(functools.partial(kernel, 1.0 / math.sqrt(total), 1.0 / to...  121 us
    unnamed x1, local copies, waits for them, and re-layouts  4.64 us

profile of v1, /device:TPU:1, one launch (start us, length us, event | category | flops | bytes accessed | tf_op | source)
XLA Modules:
  0.0 126.7 jit_solution(16878954272506463642)
XLA Ops:
  0.7 121.4 %shard_map.46 = bf16[2048,1024]{1,0:T(8,128)(2,1)} custom-call(s32[1,1]{1,0:T(1,128)S(6)} %copy.6.code_ref, bf16[4,2,16,2048]{3,2,1,0:T(8,128)(2,1)} %bitcast.2, bf16[2,4,2,16,1024]{4,3,2,1,0:T(8,128)(2,1)} %bitcast.3, bf16[2048,1024]{1,0:T(8,128)(2,1)} %w_hbm.1), custom_call_target="tpu_custom_call" | custom-call | tf_op jit(solution)/shard_map/pallas_call | solution.py:403
  122.1 4.6 %copy.7 = bf16[2048,1024]{1,0:T(8,128)(2,1)} copy(bf16[2048,1024]{1,0:T(8,128)(2,1)} %shard_map.46) | data formatting | bytes 8388608

commit v2 on v1

v2 whole, which is shorter than its diff:
```python
import functools
import math

import jax
import jax.numpy as jnp
from jax import lax
from jax.experimental import pallas as pl
from jax.experimental.pallas import tpu as pltpu
from jax.sharding import PartitionSpec as P

MESH = pl.DeviceIdType.MESH
BF = jnp.bfloat16
F32 = jnp.float32
AVG = 128
SUB = 16
ERR, TAN = 0, 1
GROUPS = ((0, 2), (2, 5), (5, 8), (8, 11), (11, 14), (14, 16))


def unit(slot, part):
    return part if slot == 0 else 2 + 3 * part + slot - 1 if slot < 4 else 2 * slot + part


SLOTS = {unit(slot, part): (slot, part) for slot in range(8) for part in range(2)}


def wrapped(value):
    return (value + 2**31) % 2**32 - 2**31


def remote(src, dst, send, recv, peer):
    return pltpu.make_async_remote_copy(
        src_ref=src, dst_ref=dst, send_sem=send, recv_sem=recv,
        device_id=peer, device_id_type=MESH,
    )


def kernel(
    grad_scale, curv_scale, code_ref, x_hbm, y_hbm, w_hbm, out_hbm,
    xg, w, y, pt, own, hold_p, hold_m, sb_p, sb_m, s2_p, s2_m, rb_p, rb_m, r2_p, r2_m,
    et, g_own, m_own, g_send, m_send, g_recv, m_recv, h_send, n_send, h_recv, n_recv, stage,
    load_sem, xs, xr, rs_s, rs_r, ag_s, ag_r, co_s, co_r, zs, zr, fs, fr, ls,
):
    rep, row, col = lax.axis_index("rep"), lax.axis_index("row"), lax.axis_index("col")
    plane, ypos = row // 4, row % 4
    core = rep % 2
    right, left = (col + 1) % 4, (col + 3) % 4
    to_right, to_left = {"col": right}, {"col": left}
    up, down = {"row": plane * 4 + (ypos + 1) % 4}, {"row": plane * 4 + (ypos + 3) % 4}
    across = {"row": (row + 4) % 8}
    twin = {"rep": rep - core + (1 - core)}
    zmate = {"rep": (rep + 2) % 4}
    rows, cols = w.shape
    nc = cols // AVG
    half = rows // 2
    mid = cols // 2

    loads = [
        pltpu.make_async_copy(x_hbm, xg.at[:, 0:2], load_sem.at[0]),
        pltpu.make_async_copy(w_hbm, w, load_sem.at[1]),
        pltpu.make_async_copy(y_hbm, y, load_sem.at[2]),
    ]
    for load in loads:
        load.start()

    barrier = pltpu.get_barrier_semaphore()
    peers = (to_right, to_left, up, down, across, twin, zmate)
    for peer in peers:
        pl.semaphore_signal(barrier, inc=1, device_id=peer, device_id_type=MESH)
    pl.semaphore_wait(barrier, len(peers))
    loads[0].wait()

    sent = []

    def pass_on(slot, part, peer, landing, share=None):
        k = len(sent)
        lo, hi, semaphore = (0, 4, unit(landing, part)) if share is None else (2 * share, 2 * share + 2, 16 + share)
        copy = remote(
            xg.at[lo:hi, unit(slot, part)], xg.at[lo:hi, unit(landing, part)], xs.at[k], xr.at[semaphore], peer
        )
        copy.start()
        sent.append(copy)

    def arrived(slot, part, share=None):
        u = unit(slot, part)
        lo, hi, semaphore = (0, 4, u) if share is None else (2 * share, 2 * share + 2, 16 + share)
        remote(xg.at[lo:hi, u], xg.at[lo:hi, u], xs.at[0], xr.at[semaphore], across).wait_recv()

    for part in range(2):
        pass_on(0, part, across, 1)
        pass_on(0, part, up, 3)
        pass_on(0, part, down, 2)

    loads[1].wait()
    loads[2].wait()

    slot_rows = []
    other = 1 - plane
    for pl_, dy in ((plane, 0), (other, 0), (plane, 1), (plane, 3), (plane, 2), (other, 1), (other, 3), (other, 2)):
        slot_rows.append(pl_ * 4 + (ypos + dy) % 4)

    def members(group):
        lo, hi = GROUPS[group]
        pieces = [xg[(col + k) % 4, lo:hi].reshape((hi - lo) * SUB, rows) for k in range(4)]
        return jnp.concatenate(pieces, axis=0)

    def put(ref, kind, group, lanes, value):
        lo, hi = GROUPS[group]
        ref[kind, lo:hi, :, lanes] = value.reshape(hi - lo, SUB, value.shape[-1])

    def get(ref, kind, group, lanes):
        lo, hi = GROUPS[group]
        value = ref[kind, lo:hi, :, lanes]
        return value.reshape((hi - lo) * SUB, value.shape[-1])

    BLOCK = 256

    def sums_of(kind, group, lanes):
        n = (GROUPS[group][1] - GROUPS[group][0]) * SUB
        if kind == TAN:
            sums = lax.dot_general(
                members(group), pt[lanes, :], (((1,), (1,)), ((), ())), preferred_element_type=F32
            )
            return [sums[k * n:(k + 1) * n] for k in range(4)]
        sums = jnp.dot(members(group), w[:, lanes], preferred_element_type=F32)
        parts = []
        for k in range(4):
            wanted = []
            for u in range(*GROUPS[group]):
                s, h = SLOTS[u]
                mine = (slot_rows[s] // 2 == col).astype(F32)
                wanted.append(y[slot_rows[s] % 2, (col + k) % 4, h, :, lanes].astype(F32) * mine)
            parts.append(sums[k * n:(k + 1) * n] - jnp.concatenate(wanted, axis=0))
        return parts

    def partial(kind, group):
        def low(j, carry):
            lanes = pl.ds(pl.multiple_of(j * BLOCK, BLOCK), BLOCK)
            parts = sums_of(kind, group, lanes)
            put(own, kind, group, lanes, parts[0])
            put(hold_p, kind, group, lanes, parts[1])
            put(sb_p, kind, group, lanes, parts[2].astype(BF))
            put(sb_m, kind, group, lanes, parts[3].astype(BF))
            return carry

        def high(j, carry):
            lanes = pl.ds(pl.multiple_of(j * BLOCK + mid, BLOCK), BLOCK)
            parts = sums_of(kind, group, lanes)
            put(own, kind, group, lanes, parts[0])
            put(sb_p, kind, group, lanes, parts[1].astype(BF))
            put(sb_m, kind, group, lanes, parts[2].astype(BF))
            put(hold_m, kind, group, pl.ds(pl.multiple_of(j * BLOCK, BLOCK), BLOCK), parts[3])
            return carry

        lax.fori_loop(0, mid // BLOCK, low, 0)
        lax.fori_loop(0, mid // BLOCK, high, 0)
        for copy in first_hop(kind, group):
            copy.start()

    def hop(kind, group, number, source, target, peer):
        lo, hi = GROUPS[group]
        return remote(
            source.at[kind, lo:hi], target.at[kind, lo:hi],
            rs_s.at[kind, number, group], rs_r.at[kind, number, group], peer,
        )

    def first_hop(kind, group):
        return [hop(kind, group, 0, sb_p, rb_p, to_right), hop(kind, group, 1, sb_m, rb_m, to_left)]

    def second_hop(kind, group):
        return [hop(kind, group, 2, s2_p, r2_p, to_right), hop(kind, group, 3, s2_m, r2_m, to_left)]

    def relay(kind, group):
        low, high, every = slice(0, mid), slice(mid, cols), slice(0, mid)
        first, second = first_hop(kind, group), second_hop(kind, group)
        first[0].wait_recv()
        put(s2_p, kind, group, every, (get(hold_p, kind, group, every) + get(rb_p, kind, group, low).astype(F32)).astype(BF))
        second[0].start()
        first[1].wait_recv()
        put(s2_m, kind, group, every, (get(hold_m, kind, group, every) + get(rb_m, kind, group, high).astype(F32)).astype(BF))
        second[1].start()

    def reduced(kind):
        for group in range(len(GROUPS)):
            for copy in second_hop(kind, group):
                copy.wait_recv()

    def probe_signs():
        code = code_ref[0, 0] * 1013904223
        lane = lax.broadcasted_iota(jnp.int32, (SUB, 512), 1) * 1664525
        sub = lax.broadcasted_iota(jnp.int32, (SUB, 512), 0) * 22695477
        base = lane + sub + code

        def step(j, carry):
            for i in range(rows // 512):
                mixed = base + (j * (SUB * 22695477) + wrapped(i * 512 * 1664525))
                mixed = mixed ^ mixed >> 15 & 131071
                mixed = mixed * 1274126177
                mixed = mixed ^ mixed >> 13 & 524287
                parity = mixed >> 7 & 1
                pt[pl.ds(pl.multiple_of(j * SUB, SUB), SUB), i * 512:(i + 1) * 512] = (
                    (1 - 2 * parity).astype(F32).astype(BF)
                )
            return carry

        lax.fori_loop(0, cols // SUB, step, 0)

    partial(ERR, 0)
    probe_signs()
    partial(TAN, 0)

    for s in (1, 2, 3):
        arrived(s, 0)
    pass_on(3, 0, up, 4)
    pass_on(2, 0, across, 5)
    pass_on(1, 0, up, 6)
    partial(ERR, 1)
    relay(ERR, 0)
    partial(TAN, 1)
    relay(TAN, 0)

    for s in (1, 2, 3):
        arrived(s, 1)
    pass_on(2, 1, down, 4)
    pass_on(3, 1, across, 6)
    pass_on(1, 1, down, 5)
    partial(ERR, 2)
    relay(ERR, 1)
    partial(TAN, 2)
    relay(TAN, 1)

    arrived(4, 0)
    pass_on(4, 0, across, 7)
    arrived(5, 0)
    arrived(4, 1)
    partial(ERR, 3)
    relay(ERR, 2)
    partial(TAN, 3)
    relay(TAN, 2)

    arrived(6, 0)
    arrived(6, 1)
    pass_on(6, 1, up, 7, 0)
    arrived(5, 1)
    pass_on(5, 1, down, 7, 1)
    partial(ERR, 4)
    relay(ERR, 3)
    relay(TAN, 3)

    arrived(7, 0)
    arrived(7, 1, 0)
    arrived(7, 1, 1)
    partial(ERR, 5)
    relay(ERR, 4)
    partial(TAN, 4)
    relay(ERR, 5)
    partial(TAN, 5)
    relay(TAN, 4)
    reduced(ERR)

    def own_block(kind, c):
        area = et.at[kind, c, col]
        return [
            remote(area, area, ag_s.at[kind, 0, c], ag_r.at[kind, 0, c], to_right),
            remote(area, area, ag_s.at[kind, 1, c], ag_r.at[kind, 1, c], to_left),
        ]

    def far_block(kind, c):
        first, second = slice(0, AVG // 2), slice(AVG // 2, AVG)
        low, high = et.at[kind, c, left, first], et.at[kind, c, right, second]
        return [
            remote(low, low, ag_s.at[kind, 2, c], ag_r.at[kind, 2, c], to_right),
            remote(high, high, ag_s.at[kind, 3, c], ag_r.at[kind, 3, c], to_left),
        ]

    def twin_block(c):
        return [remote(g_send.at[c], g_recv.at[c], co_s.at[0, c], co_r.at[0, c], twin)]

    def twin_means(c):
        return [remote(m_send.at[c], m_recv.at[c], co_s.at[1, c], co_r.at[1, c], twin)]

    def z_block(c):
        return [remote(h_send.at[c], h_recv.at[c], zs.at[0, c], zr.at[0, c], zmate)]

    def z_means(c):
        return [remote(n_send.at[c], n_recv.at[c], zs.at[1, c], zr.at[1, c], zmate)]

    def result(c):
        area = out_hbm.at[
            pl.ds(pl.multiple_of(core * half, half), half), pl.ds(pl.multiple_of(c * AVG, AVG), AVG)
        ]
        return remote(stage.at[c], area, fs.at[c], fr.at[c], twin), pltpu.make_async_copy(
            stage.at[c], area, ls.at[c]
        )

    units = own.shape[1]
    tokens = units * SUB

    def share(kind, c):
        lanes = pl.ds(pl.multiple_of(c * AVG, AVG), AVG)
        within = pl.ds(pl.multiple_of(c % (nc // 2) * AVG, AVG), AVG)

        def all_of(ref, lanes):
            return ref[kind, :, :, lanes].reshape(tokens, AVG).astype(F32)

        def finish(direct, relayed):
            total = all_of(own, lanes) + all_of(direct, lanes) + all_of(relayed, within)
            et[kind, c, col] = total.T.astype(BF)

        @pl.when(c < nc // 2)
        def _():
            finish(rb_m, r2_p)

        @pl.when(c >= nc // 2)
        def _():
            finish(rb_p, r2_m)

        for copy in own_block(kind, c):
            copy.start()

    def far_share(kind, c):
        own_copies, far_copies = own_block(kind, c), far_block(kind, c)
        for mine, theirs in zip(own_copies, far_copies):
            mine.wait_recv()
            theirs.start()

    PART = 512

    def whole(kind, c):
        for copy in far_block(kind, c):
            copy.wait_recv()
        return jnp.concatenate([et[kind, c, k] for k in range(4)], axis=1)

    def product(block, owner, p):
        start = pl.multiple_of(owner * half + p * PART, PART)
        x = xg[:, :, :, pl.ds(start, PART)].reshape(4 * tokens, PART)
        return jnp.dot(block, x, preferred_element_type=F32), pl.ds(start, PART)

    def contract(c):
        errors = whole(ERR, c)
        for p in range(half // PART):
            g_send[c, :, p * PART:(p + 1) * PART] = (product(errors, 1 - core, p)[0] * grad_scale).astype(BF)
        for copy in twin_block(c):
            copy.start()
        for p in range(half // PART):
            g_own[c % 2, :, p * PART:(p + 1) * PART] = product(errors, core, p)[0] * grad_scale

    def curvature(c):
        tangents = whole(TAN, c)
        signs = pl.ds(pl.multiple_of(c * AVG, AVG), AVG)

        def means(ref, owner):
            for p in range(half // PART):
                sums, lanes = product(tangents, owner, p)
                mean = jnp.sum(sums * pt[signs, lanes].astype(F32), axis=0, keepdims=True) * curv_scale
                for k in range(PART // 128):
                    at = p * (PART // 128) + k
                    ref[at:at + 1, :] = mean[:, k * 128:(k + 1) * 128]

        means(m_send.at[c], 1 - core)
        for copy in twin_means(c):
            copy.start()
        means(m_own.at[c % 2], core)

    def reduce_twin(c):
        for copy in twin_block(c):
            copy.wait_recv()
        h_send[c] = (g_own[c % 2] + g_recv[c].astype(F32)).astype(BF)
        for copy in z_block(c):
            copy.start()

    def reduce_means(c):
        for copy in twin_means(c):
            copy.wait_recv()
        n_send[c] = m_own[c % 2] + m_recv[c]
        for copy in z_means(c):
            copy.start()

    def divide(c):
        for copy in z_block(c) + z_means(c):
            copy.wait_recv()
        means = n_send[c] + n_recv[c]
        denom = jnp.maximum(jnp.abs(means), 0.25)
        for k in range(half // 128):
            lanes = slice(k * 128, (k + 1) * 128)
            gradient = h_send[c, :, lanes].astype(F32) + h_recv[c, :, lanes].astype(F32)
            stage[c, lanes, :] = (gradient / denom[k:k + 1, :]).T.astype(BF)
        for copy in result(c):
            copy.start()

    LAG = 7

    def main(t, carry):
        def when(lag):
            return pl.when((t >= lag) & (t < nc + lag))

        @when(0)
        def _():
            share(ERR, t)

        @pl.when(t == 0)
        def _():
            relay(TAN, 5)

        @when(1)
        def _():
            far_share(ERR, t - 1)

        @when(2)
        def _():
            contract(t - 2)

        @pl.when(t == 2)
        def _():
            reduced(TAN)

        @when(2)
        def _():
            share(TAN, t - 2)
            reduce_twin(t - 2)

        @when(3)
        def _():
            far_share(TAN, t - 3)

        @when(4)
        def _():
            curvature(t - 4)

        @when(LAG)
        def _():
            divide(t - LAG)

        @when(4)
        def _():
            reduce_means(t - 4)

        return carry

    lax.fori_loop(0, nc + LAG, main, 0)

    for copy in sent:
        copy.wait_send()
    for kind in (ERR, TAN):
        for group in range(len(GROUPS)):
            for copy in first_hop(kind, group) + second_hop(kind, group):
                copy.wait_send()

    def drain(c, carry):
        for kind in (ERR, TAN):
            for copy in own_block(kind, c) + far_block(kind, c):
                copy.wait_send()
        for copy in twin_block(c) + twin_means(c) + z_block(c) + z_means(c):
            copy.wait_send()
        there, here = result(c)
        there.wait()
        here.wait()
        return carry

    lax.fori_loop(0, nc, drain, 0)


def shards(activations, target, weight, probe_codes):
    share, rows = activations.shape
    cols = weight.shape[1]
    nc = cols // AVG
    tokens_micro = share * lax.axis_size("row")
    total = tokens_micro * lax.axis_size("rep")
    x = activations.reshape(4, 2, SUB, rows)
    y = target.reshape(2, 4, 2, SUB, cols)
    half = rows // 2
    vmem = pltpu.VMEM
    dma = pltpu.SemaphoreType.DMA
    return pl.pallas_call(
        functools.partial(kernel, 1.0 / math.sqrt(total), 1.0 / total / AVG),
        out_shape=jax.ShapeDtypeStruct((rows, cols), BF),
        in_specs=[pl.BlockSpec(memory_space=pltpu.SMEM)] + [pl.BlockSpec(memory_space=pl.ANY)] * 3,
        out_specs=pl.BlockSpec(memory_space=pl.ANY),
        scratch_shapes=[
            vmem((4, 16, SUB, rows), BF),
            vmem((rows, cols), BF),
            vmem((2, 4, 2, SUB, cols), BF),
            vmem((cols, rows), BF),
            vmem((2, 16, SUB, cols), F32),
            vmem((2, 16, SUB, cols // 2), F32),
            vmem((2, 16, SUB, cols // 2), F32),
            vmem((2, 16, SUB, cols), BF),
            vmem((2, 16, SUB, cols), BF),
            vmem((2, 16, SUB, cols // 2), BF),
            vmem((2, 16, SUB, cols // 2), BF),
            vmem((2, 16, SUB, cols), BF),
            vmem((2, 16, SUB, cols), BF),
            vmem((2, 16, SUB, cols // 2), BF),
            vmem((2, 16, SUB, cols // 2), BF),
            vmem((2, nc, 4, AVG, 256), BF),
            vmem((2, AVG, half), F32),
            vmem((2, 8, 128), F32),
            vmem((nc, AVG, half), BF),
            vmem((nc, 8, 128), F32),
            vmem((nc, AVG, half), BF),
            vmem((nc, 8, 128), F32),
            vmem((nc, AVG, half), BF),
            vmem((nc, 8, 128), F32),
            vmem((nc, AVG, half), BF),
            vmem((nc, 8, 128), F32),
            vmem((nc, half, AVG), BF),
            dma((3,)),
            dma((15,)),
            dma((18,)),
            dma((2, 4, 6)),
            dma((2, 4, 6)),
            dma((2, 4, nc)),
            dma((2, 4, nc)),
            dma((2, nc)),
            dma((2, nc)),
            dma((2, nc)),
            dma((2, nc)),
            dma((nc,)),
            dma((nc,)),
            dma((nc,)),
        ],
        compiler_params=pltpu.CompilerParams(
            collective_id=0, has_side_effects=True, vmem_limit_bytes=62 * 1024 * 1024
        ),
    )(probe_codes, x, y, weight)


def solution(mesh):
    placed = (P(("rep", "row"), "col"), P(("rep", "col"), "row"), P("col", "row"), P("col", "row"))
    return jax.shard_map(
        shards, mesh=mesh, in_specs=placed, out_specs=P("col", "row"), check_vma=False
    )
```

time: 127 us -> 116 us (0.913)
  Pallas kernels: 121 us -> 110 us
    pallas_call x1, Pallas kernels: 121 us -> 110 us  [shards(): pl.pallas_call(functools.partial(kernel, 1.0 / math.sqrt(total), 1.0 / to...]
where the time goes in v2:
time: 116 us
  Pallas kernels  110 us (95%)
  local copies, waits for them, and re-layouts  4.64 us (4%)
    pallas_call x1, Pallas kernels, shards(): pl.pallas_call(functools.partial(kernel, 1.0 / math.sqrt(total), 1.0 / to...  110 us
    unnamed x1, local copies, waits for them, and re-layouts  4.64 us

profile of v2, /device:TPU:1, one launch (start us, length us, event | category | flops | bytes accessed | tf_op | source)
XLA Modules:
  0.0 115.7 jit_solution(11403083232018807779)
XLA Ops:
  0.7 110.4 %shard_map.46 = bf16[2048,1024]{1,0:T(8,128)(2,1)} custom-call(s32[1,1]{1,0:T(1,128)S(6)} %copy.6.code_ref, bf16[4,2,16,2048]{3,2,1,0:T(8,128)(2,1)} %bitcast.2, bf16[2,4,2,16,1024]{4,3,2,1,0:T(8,128)(2,1)} %bitcast.3, bf16[2048,1024]{1,0:T(8,128)(2,1)} %w_hbm.1), custom_call_target="tpu_custom_call" | custom-call | tf_op jit(solution)/shard_map/pallas_call | solution.py:474
  111.1 4.6 %copy.7 = bf16[2048,1024]{1,0:T(8,128)(2,1)} copy(bf16[2048,1024]{1,0:T(8,128)(2,1)} %shard_map.46) | data formatting | bytes 8388608

commit v3 on v2

--- a/solution.py
+++ b/solution.py
@@ -36,16 +36,16 @@
 
 
 def kernel(
-    grad_scale, curv_scale, code_ref, x_hbm, y_hbm, w_hbm, out_hbm,
+    grad_scale, curv_scale, code_ref, x_hbm, y_hbm, w_hbm, out,
     xg, w, y, pt, own, hold_p, hold_m, sb_p, sb_m, s2_p, s2_m, rb_p, rb_m, r2_p, r2_m,
-    et, g_own, m_own, g_send, m_send, g_recv, m_recv, h_send, n_send, h_recv, n_recv, stage,
-    load_sem, xs, xr, rs_s, rs_r, ag_s, ag_r, co_s, co_r, zs, zr, fs, fr, ls,
+    et, g_own, m_own, g_send, m_send, g_recv, m_recv, h_send, n_send, h_recv, n_recv,
+    load_sem, xs, xr, rs_s, rs_r, ag_s, ag_r, co_s, co_r, zs, zr, fs, fr,
 ):
     rep, row, col = lax.axis_index("rep"), lax.axis_index("row"), lax.axis_index("col")
     plane, ypos = row // 4, row % 4
     core = rep % 2
     right, left = (col + 1) % 4, (col + 3) % 4
-    to_right, to_left = {"col": right}, {"col": left}
+    to_right, to_left, to_far = {"col": right}, {"col": left}, {"col": (col + 2) % 4}
     up, down = {"row": plane * 4 + (ypos + 1) % 4}, {"row": plane * 4 + (ypos + 3) % 4}
     across = {"row": (row + 4) % 8}
     twin = {"rep": rep - core + (1 - core)}
@@ -64,7 +64,7 @@
         load.start()
 
     barrier = pltpu.get_barrier_semaphore()
-    peers = (to_right, to_left, up, down, across, twin, zmate)
+    peers = (to_right, to_left, to_far, up, down, across, twin, zmate)
     for peer in peers:
         pl.semaphore_signal(barrier, inc=1, device_id=peer, device_id_type=MESH)
     pl.semaphore_wait(barrier, len(peers))
@@ -133,7 +133,7 @@
             parts.append(sums[k * n:(k + 1) * n] - jnp.concatenate(wanted, axis=0))
         return parts
 
-    def partial(kind, group):
+    def partial(kind, group, hold=False):
         def low(j, carry):
             lanes = pl.ds(pl.multiple_of(j * BLOCK, BLOCK), BLOCK)
             parts = sums_of(kind, group, lanes)
@@ -154,8 +154,9 @@
 
         lax.fori_loop(0, mid // BLOCK, low, 0)
         lax.fori_loop(0, mid // BLOCK, high, 0)
-        for copy in first_hop(kind, group):
-            copy.start()
+        if not hold:
+            for copy in first_hop(kind, group):
+                copy.start()
 
     def hop(kind, group, number, source, target, peer):
         lo, hi = GROUPS[group]
@@ -180,10 +181,59 @@
         put(s2_m, kind, group, every, (get(hold_m, kind, group, every) + get(rb_m, kind, group, high).astype(F32)).astype(BF))
         second[1].start()
 
-    def reduced(kind):
-        for group in range(len(GROUPS)):
-            for copy in second_hop(kind, group):
-                copy.wait_recv()
+    LAST = len(GROUPS) - 1
+
+    def lane_hop(kind, number, source, target, peer, lanes):
+        lo, hi = GROUPS[LAST]
+        return remote(
+            source.at[kind, lo:hi, :, lanes], target.at[kind, lo:hi, :, lanes],
+            rs_s.at[kind, number, LAST], rs_r.at[kind, number, LAST], peer,
+        )
+
+    def straight(kind, high):
+        lanes = slice(mid, cols) if high else slice(0, mid)
+        far = hop(kind, LAST, 3, s2_m, r2_m, to_far) if high else hop(kind, LAST, 2, s2_p, r2_p, to_far)
+        return [
+            lane_hop(kind, 4 if high else 0, sb_p, rb_p, to_right, lanes),
+            lane_hop(kind, 5 if high else 1, sb_m, rb_m, to_left, lanes),
+            far,
+        ]
+
+    def partial_last(kind, hold=False):
+        def low(j, carry):
+            lanes = pl.ds(pl.multiple_of(j * BLOCK, BLOCK), BLOCK)
+            parts = sums_of(kind, LAST, lanes)
+            put(own, kind, LAST, lanes, parts[0])
+            put(sb_p, kind, LAST, lanes, parts[1].astype(BF))
+            put(s2_p, kind, LAST, lanes, parts[2].astype(BF))
+            put(sb_m, kind, LAST, lanes, parts[3].astype(BF))
+            return carry
+
+        def high(j, carry):
+            lanes = pl.ds(pl.multiple_of(j * BLOCK + mid, BLOCK), BLOCK)
+            parts = sums_of(kind, LAST, lanes)
+            put(own, kind, LAST, lanes, parts[0])
+            put(sb_p, kind, LAST, lanes, parts[1].astype(BF))
+            put(s2_m, kind, LAST, pl.ds(pl.multiple_of(j * BLOCK, BLOCK), BLOCK), parts[2].astype(BF))
+            put(sb_m, kind, LAST, lanes, parts[3].astype(BF))
+            return carry
+
+        lax.fori_loop(0, mid // BLOCK, low, 0)
+        if not hold:
+            for copy in straight(kind, False):
+                copy.start()
+        lax.fori_loop(0, mid // BLOCK, high, 0)
+        if not hold:
+            for copy in straight(kind, True):
+                copy.start()
+
+    def reduced(kind, high):
+        for group in range(LAST):
+            second_hop(kind, group)[1 if high else 0].wait_recv()
+        for copy in straight(kind, high):
+            copy.wait_recv()
+        lanes, ref = (slice(mid, cols), rb_m) if high else (slice(0, mid), rb_p)
+        put(own, kind, LAST, lanes, get(own, kind, LAST, lanes) + get(ref, kind, LAST, lanes).astype(F32))
 
     def probe_signs():
         code = code_ref[0, 0] * 1013904223
@@ -235,7 +285,7 @@
     arrived(4, 1)
     partial(ERR, 3)
     relay(ERR, 2)
-    partial(TAN, 3)
+    partial(TAN, 3, hold=True)
     relay(TAN, 2)
 
     arrived(6, 0)
@@ -245,18 +295,14 @@
     pass_on(5, 1, down, 7, 1)
     partial(ERR, 4)
     relay(ERR, 3)
-    relay(TAN, 3)
 
     arrived(7, 0)
     arrived(7, 1, 0)
     arrived(7, 1, 1)
-    partial(ERR, 5)
     relay(ERR, 4)
-    partial(TAN, 4)
-    relay(ERR, 5)
-    partial(TAN, 5)
-    relay(TAN, 4)
-    reduced(ERR)
+    partial_last(ERR)
+    partial(TAN, 4, hold=True)
+    reduced(ERR, False)
 
     def own_block(kind, c):
         area = et.at[kind, c, col]
@@ -273,25 +319,34 @@
             remote(high, high, ag_s.at[kind, 3, c], ag_r.at[kind, 3, c], to_left),
         ]
 
-    def twin_block(c):
-        return [remote(g_send.at[c], g_recv.at[c], co_s.at[0, c], co_r.at[0, c], twin)]
+    def first_block(c):
+        first, second = slice(0, AVG // 2), slice(AVG // 2, AVG)
+        low, high = et.at[ERR, c, col, first], et.at[ERR, c, col, second]
+        return own_block(ERR, c) + [
+            remote(low, low, ag_s.at[ERR, 2, c], ag_r.at[ERR, 2, c], to_far),
+            remote(high, high, ag_s.at[ERR, 3, c], ag_r.at[ERR, 3, c], to_far),
+        ]
+
+    PARTS = 2
+    PART = half // PARTS
+
+    def twin_block(c, p):
+        return remote(g_send.at[c, p], g_recv.at[c, p], co_s.at[p, c], co_r.at[p, c], twin)
 
     def twin_means(c):
-        return [remote(m_send.at[c], m_recv.at[c], co_s.at[1, c], co_r.at[1, c], twin)]
-
-    def z_block(c):
-        return [remote(h_send.at[c], h_recv.at[c], zs.at[0, c], zr.at[0, c], zmate)]
+        return remote(m_send.at[c], m_recv.at[c], co_s.at[PARTS, c], co_r.at[PARTS, c], twin)
+
+    def z_block(c, p):
+        return remote(h_send.at[c, p], h_recv.at[c, p], zs.at[p, c], zr.at[p, c], zmate)
 
     def z_means(c):
-        return [remote(n_send.at[c], n_recv.at[c], zs.at[1, c], zr.at[1, c], zmate)]
-
-    def result(c):
-        area = out_hbm.at[
-            pl.ds(pl.multiple_of(core * half, half), half), pl.ds(pl.multiple_of(c * AVG, AVG), AVG)
+        return remote(n_send.at[c], n_recv.at[c], zs.at[PARTS, c], zr.at[PARTS, c], zmate)
+
+    def result(c, p):
+        area = out.at[
+            pl.ds(pl.multiple_of(core * half + p * PART, PART), PART), pl.ds(pl.multiple_of(c * AVG, AVG), AVG)
         ]
-        return remote(stage.at[c], area, fs.at[c], fr.at[c], twin), pltpu.make_async_copy(
-            stage.at[c], area, ls.at[c]
-        )
+        return remote(area, area, fs.at[p, c], fr.at[p, c], twin)
 
     units = own.shape[1]
     tokens = units * SUB
@@ -315,6 +370,8 @@
         def _():
             finish(rb_p, r2_m)
 
+    def send_share(kind, c):
+        share(kind, c)
         for copy in own_block(kind, c):
             copy.start()
 
@@ -324,8 +381,6 @@
             mine.wait_recv()
             theirs.start()
 
-    PART = 512
-
     def whole(kind, c):
         for copy in far_block(kind, c):
             copy.wait_recv()
@@ -336,128 +391,192 @@
         x = xg[:, :, :, pl.ds(start, PART)].reshape(4 * tokens, PART)
         return jnp.dot(block, x, preferred_element_type=F32), pl.ds(start, PART)
 
-    def contract(c):
-        errors = whole(ERR, c)
-        for p in range(half // PART):
-            g_send[c, :, p * PART:(p + 1) * PART] = (product(errors, 1 - core, p)[0] * grad_scale).astype(BF)
-        for copy in twin_block(c):
-            copy.start()
-        for p in range(half // PART):
-            g_own[c % 2, :, p * PART:(p + 1) * PART] = product(errors, core, p)[0] * grad_scale
-
-    def curvature(c):
-        tangents = whole(TAN, c)
-        signs = pl.ds(pl.multiple_of(c * AVG, AVG), AVG)
-
-        def means(ref, owner):
-            for p in range(half // PART):
-                sums, lanes = product(tangents, owner, p)
-                mean = jnp.sum(sums * pt[signs, lanes].astype(F32), axis=0, keepdims=True) * curv_scale
-                for k in range(PART // 128):
-                    at = p * (PART // 128) + k
-                    ref[at:at + 1, :] = mean[:, k * 128:(k + 1) * 128]
-
-        means(m_send.at[c], 1 - core)
-        for copy in twin_means(c):
-            copy.start()
-        means(m_own.at[c % 2], core)
-
-    def reduce_twin(c):
-        for copy in twin_block(c):
-            copy.wait_recv()
-        h_send[c] = (g_own[c % 2] + g_recv[c].astype(F32)).astype(BF)
-        for copy in z_block(c):
-            copy.start()
-
-    def reduce_means(c):
-        for copy in twin_means(c):
-            copy.wait_recv()
-        n_send[c] = m_own[c % 2] + m_recv[c]
-        for copy in z_means(c):
-            copy.start()
+    def contract(e, t):
+        blocks = [] if e is None else [whole(ERR, e)]
+        blocks += [] if t is None else [whole(TAN, t)]
+        both = jnp.concatenate(blocks, axis=0)
+
+        def means(sums, lanes, ref, p):
+            signs = pl.ds(pl.multiple_of(t * AVG, AVG), AVG)
+            mean = jnp.sum(sums * pt[signs, lanes].astype(F32), axis=0, keepdims=True) * curv_scale
+            for k in range(PART // 128):
+                at = p * (PART // 128) + k
+                ref[at:at + 1, :] = mean[:, k * 128:(k + 1) * 128]
+
+        for p in range(PARTS):
+            sums, lanes = product(both, 1 - core, p)
+            if e is not None:
+                g_send[e, p] = (sums[:AVG] * grad_scale).astype(BF)
+                twin_block(e, p).start()
+            if t is not None:
+                means(sums[-AVG:], lanes, m_send.at[t], p)
+        if t is not None:
+            twin_means(t).start()
+        for p in range(PARTS):
+            sums, lanes = product(both, core, p)
+            if e is not None:
+                g_own[p] = sums[:AVG] * grad_scale
+            if t is not None:
+                means(sums[-AVG:], lanes, m_own, p)
+
+    def reduce_means(t):
+        twin_means(t).wait_recv()
+        n_send[t] = m_own[...] + m_recv[t]
+        z_means(t).start()
+
+    def reduce_twin(e):
+        for p in range(PARTS):
+            twin_block(e, p).wait_recv()
+            h_send[e, p] = (g_own[p] + g_recv[e, p].astype(F32)).astype(BF)
 
     def divide(c):
-        for copy in z_block(c) + z_means(c):
-            copy.wait_recv()
+        z_means(c).wait_recv()
         means = n_send[c] + n_recv[c]
         denom = jnp.maximum(jnp.abs(means), 0.25)
-        for k in range(half // 128):
-            lanes = slice(k * 128, (k + 1) * 128)
-            gradient = h_send[c, :, lanes].astype(F32) + h_recv[c, :, lanes].astype(F32)
-            stage[c, lanes, :] = (gradient / denom[k:k + 1, :]).T.astype(BF)
-        for copy in result(c):
-            copy.start()
-
-    LAG = 7
+        columns = pl.ds(pl.multiple_of(c * AVG, AVG), AVG)
+        for p in range(PARTS):
+            z_block(c, p).wait_recv()
+            for k in range(PART // 128):
+                lanes = slice(k * 128, (k + 1) * 128)
+                at = p * (PART // 128) + k
+                gradient = h_send[c, p, :, lanes].astype(F32) + h_recv[c, p, :, lanes].astype(F32)
+                out[pl.ds(pl.multiple_of(core * half + at * 128, 128), 128), columns] = (
+                    gradient / denom[at:at + 1, :]
+                ).T.astype(BF)
+            result(c, p).start()
+
+    def z_start(c):
+        for p in range(PARTS):
+            z_block(c, p).start()
+
+    share(ERR, 0)
+    for copy in first_block(0):
+        copy.start()
+    send_share(ERR, 1)
+    send_share(ERR, 2)
+    for copy in first_hop(TAN, 3):
+        copy.start()
+    partial_last(TAN, hold=True)
+    for copy in own_block(ERR, 0):
+        copy.wait_recv()
+    contract(0, None)
+    far_share(ERR, 1)
+    send_share(ERR, 3)
+    reduce_twin(0)
+    z_start(0)
+    for copy in first_hop(TAN, 4):
+        copy.start()
+    relay(TAN, 3)
+
+    BACK, LAG = 5, 8
 
     def main(t, carry):
         def when(lag):
             return pl.when((t >= lag) & (t < nc + lag))
 
-        @when(0)
-        def _():
-            share(ERR, t)
-
-        @pl.when(t == 0)
-        def _():
-            relay(TAN, 5)
-
-        @when(1)
-        def _():
-            far_share(ERR, t - 1)
-
-        @when(2)
-        def _():
-            contract(t - 2)
+        @pl.when(t + 1 < nc)
+        def _():
+            far_share(ERR, t + 1)
+
+        @when(BACK - 1)
+        def _():
+            far_share(TAN, t - (BACK - 1))
+
+        @pl.when(t == 1)
+        def _():
+            for copy in straight(TAN, False) + straight(TAN, True):
+                copy.start()
+            reduced(ERR, True)
+
+        @pl.when(t + 3 < nc)
+        def _():
+            send_share(ERR, t + 3)
+
+        @pl.when((t >= 3) & (t < nc + 2))
+        def _():
+            send_share(TAN, t - 2)
+
+        @pl.when(t < BACK)
+        def _():
+            contract(t, None)
+
+        @pl.when((t >= BACK) & (t < nc))
+        def _():
+            contract(t, t - BACK)
+
+        @pl.when((t >= nc) & (t < nc + BACK))
+        def _():
+            contract(None, t - BACK)
+
+        @when(BACK)
+        def _():
+            reduce_means(t - BACK)
+
+        @pl.when(t < nc)
+        def _():
+            reduce_twin(t)
+
+        @pl.when(t < 6)
+        def _():
+            z_start(t)
+
+        @pl.when((t == 7) | (t == 9))
+        def _():
+            z_start((t + 5) // 2)
+
+        @pl.when(t == 1)
+        def _():
+            relay(TAN, 4)
 
         @pl.when(t == 2)
         def _():
-            reduced(TAN)
-
-        @when(2)
-        def _():
-            share(TAN, t - 2)
-            reduce_twin(t - 2)
-
-        @when(3)
-        def _():
-            far_share(TAN, t - 3)
-
-        @when(4)
-        def _():
-            curvature(t - 4)
+            reduced(TAN, False)
+            reduced(TAN, True)
+            send_share(TAN, 0)
 
         @when(LAG)
         def _():
             divide(t - LAG)
 
-        @when(4)
-        def _():
-            reduce_means(t - 4)
-
         return carry
 
-    lax.fori_loop(0, nc + LAG, main, 0)
+    lax.fori_loop(1, nc + LAG, main, 0)
 
     for copy in sent:
         copy.wait_send()
     for kind in (ERR, TAN):
-        for group in range(len(GROUPS)):
+        for group in range(LAST):
             for copy in first_hop(kind, group) + second_hop(kind, group):
                 copy.wait_send()
+        for copy in straight(kind, False) + straight(kind, True):
+            copy.wait_send()
 
     def drain(c, carry):
         for kind in (ERR, TAN):
             for copy in own_block(kind, c) + far_block(kind, c):
                 copy.wait_send()
-        for copy in twin_block(c) + twin_means(c) + z_block(c) + z_means(c):
-            copy.wait_send()
-        there, here = result(c)
-        there.wait()
-        here.wait()
+        twin_means(c).wait_send()
+        z_means(c).wait_send()
+        for p in range(PARTS):
+            twin_block(c, p).wait_send()
+            z_block(c, p).wait_send()
+            result(c, p).wait()
         return carry
 
     lax.fori_loop(0, nc, drain, 0)
+
+
+def write_out(step, out, sems):
+    n = sems.shape[0]
+    size = step.shape[0] // n
+    copies = [
+        pltpu.make_async_copy(step.at[pl.ds(k * size, size)], out.at[pl.ds(k * size, size)], sems.at[k])
+        for k in range(n)
+    ]
+    for copy in copies:
+        copy.start()
+    for copy in copies:
+        copy.wait()
 
 
 def shards(activations, target, weight, probe_codes):
@@ -471,11 +590,11 @@
     half = rows // 2
     vmem = pltpu.VMEM
     dma = pltpu.SemaphoreType.DMA
-    return pl.pallas_call(
+    step = pl.pallas_call(
         functools.partial(kernel, 1.0 / math.sqrt(total), 1.0 / total / AVG),
-        out_shape=jax.ShapeDtypeStruct((rows, cols), BF),
-        in_specs=[pl.BlockSpec(memory_space=pltpu.SMEM)] + [pl.BlockSpec(memory_space=pl.ANY)] * 3,
-        out_specs=pl.BlockSpec(memory_space=pl.ANY),
+        out_shape=pltpu.VMEM((rows, cols), BF),
+        in_specs=[pl.BlockSpec(memory_space=pltpu.SMEM)] + [pl.BlockSpec(memory_space=pltpu.MemorySpace.HBM)] * 3,
+        out_specs=pl.BlockSpec(memory_space=pltpu.VMEM),
         scratch_shapes=[
             vmem((4, 16, SUB, rows), BF),
             vmem((rows, cols), BF),
@@ -493,36 +612,42 @@
             vmem((2, 16, SUB, cols // 2), BF),
             vmem((2, 16, SUB, cols // 2), BF),
             vmem((2, nc, 4, AVG, 256), BF),
-            vmem((2, AVG, half), F32),
-            vmem((2, 8, 128), F32),
-            vmem((nc, AVG, half), BF),
+            vmem((2, AVG, half // 2), F32),
+            vmem((8, 128), F32),
+            vmem((nc, 2, AVG, half // 2), BF),
             vmem((nc, 8, 128), F32),
-            vmem((nc, AVG, half), BF),
+            vmem((nc, 2, AVG, half // 2), BF),
             vmem((nc, 8, 128), F32),
-            vmem((nc, AVG, half), BF),
+            vmem((nc, 2, AVG, half // 2), BF),
             vmem((nc, 8, 128), F32),
-            vmem((nc, AVG, half), BF),
+            vmem((nc, 2, AVG, half // 2), BF),
             vmem((nc, 8, 128), F32),
-            vmem((nc, half, AVG), BF),
             dma((3,)),
             dma((15,)),
             dma((18,)),
-            dma((2, 4, 6)),
-            dma((2, 4, 6)),
+            dma((2, 6, 6)),
+            dma((2, 6, 6)),
             dma((2, 4, nc)),
             dma((2, 4, nc)),
+            dma((3, nc)),
+            dma((3, nc)),
+            dma((3, nc)),
+            dma((3, nc)),
             dma((2, nc)),
             dma((2, nc)),
-            dma((2, nc)),
-            dma((2, nc)),
-            dma((nc,)),
-            dma((nc,)),
-            dma((nc,)),
         ],
         compiler_params=pltpu.CompilerParams(
-            collective_id=0, has_side_effects=True, vmem_limit_bytes=62 * 1024 * 1024
+            collective_id=0, has_side_effects=True, vmem_limit_bytes=50 * 1024 * 1024
         ),
-    )(probe_codes, x, y, weight)
+    )(probe_codes, *(pltpu.with_memory_space_constraint(v, pltpu.MemorySpace.HBM) for v in (x, y, weight)))
+    return pl.pallas_call(
+        write_out,
+        out_shape=jax.ShapeDtypeStruct((rows, cols), BF),
+        in_specs=[pl.BlockSpec(memory_space=pltpu.VMEM)],
+        out_specs=pl.BlockSpec(memory_space=pltpu.MemorySpace.HBM),
+        scratch_shapes=[dma((4,))],
+        compiler_params=pltpu.CompilerParams(vmem_limit_bytes=1024 * 1024),
+    )(step)
 
 
 def solution(mesh):

time: 116 us -> 108 us (0.931)
  local copies, waits for them, and re-layouts: 4.64 us -> 0 us
  Pallas kernels: 110 us -> 108 us
    pallas_call x1, Pallas kernels: 110 us -> 106 us  [shards(): pl.pallas_call(functools.partial(kernel, 1.0 / math.sqrt(total), 1.0 / to...]
    unnamed x1 -> x0, local copies, waits for them, and re-layouts: 4.64 us -> none
    pallas_call x0 -> x1, Pallas kernels: none -> 2.04 us  [shards(): pl.pallas_call(write_out, out_shape=jax.ShapeDtypeStruct((rows, cols), BF...]
where the time goes in v3:
time: 108 us
  Pallas kernels  108 us (100%)
    pallas_call x1, Pallas kernels, shards(): pl.pallas_call(functools.partial(kernel, 1.0 / math.sqrt(total), 1.0 / to...  106 us

profile of v3, /device:TPU:1, one launch (start us, length us, event | category | flops | bytes accessed | tf_op | source)
XLA Modules:
  0.0 108.3 jit_solution(2249995452082478774)
XLA Ops:
  0.7 105.6 %shard_map.46.step = bf16[2048,1024]{1,0:T(8,128)(2,1)S(1)} custom-call(s32[1,1]{1,0:T(1,128)S(6)} %copy.5.code_ref, bf16[4,2,16,2048]{3,2,1,0:T(8,128)(2,1)} %bitcast.2, bf16[2,4,2,16,1024]{4,3,2,1,0:T(8,128)(2,1)} %bitcast.3, bf16[2048,1024]{1,0:T(8,128)(2,1)} %w_hbm.1), custom_call_target="tpu_custom_call" | custom-call | tf_op jit(solution)/shard_map/pallas_call | solution.py:593
  106.3 2.0 %shard_map.47 = bf16[2048,1024]{1,0:T(8,128)(2,1)} custom-call(bf16[2048,1024]{1,0:T(8,128)(2,1)S(1)} %shard_map.46.step), custom_call_target="tpu_custom_call" | custom-call | tf_op jit(solution)/shard_map/pallas_call | solution.py:643

commit v4 on v3

--- a/solution.py
+++ b/solution.py
@@ -70,21 +70,17 @@
     pl.semaphore_wait(barrier, len(peers))
     loads[0].wait()
 
-    sent = []
-
     def pass_on(slot, part, peer, landing, share=None):
-        k = len(sent)
         lo, hi, semaphore = (0, 4, unit(landing, part)) if share is None else (2 * share, 2 * share + 2, 16 + share)
         copy = remote(
-            xg.at[lo:hi, unit(slot, part)], xg.at[lo:hi, unit(landing, part)], xs.at[k], xr.at[semaphore], peer
+            xg.at[lo:hi, unit(slot, part)], xg.at[lo:hi, unit(landing, part)], xs, xr.at[semaphore], peer
         )
         copy.start()
-        sent.append(copy)
 
     def arrived(slot, part, share=None):
         u = unit(slot, part)
         lo, hi, semaphore = (0, 4, u) if share is None else (2 * share, 2 * share + 2, 16 + share)
-        remote(xg.at[lo:hi, u], xg.at[lo:hi, u], xs.at[0], xr.at[semaphore], across).wait_recv()
+        remote(xg.at[lo:hi, u], xg.at[lo:hi, u], xs, xr.at[semaphore], across).wait_recv()
 
     for part in range(2):
         pass_on(0, part, across, 1)
@@ -162,7 +158,7 @@
         lo, hi = GROUPS[group]
         return remote(
             source.at[kind, lo:hi], target.at[kind, lo:hi],
-            rs_s.at[kind, number, group], rs_r.at[kind, number, group], peer,
+            rs_s.at[number], rs_r.at[kind, 4 * group + number], peer,
         )
 
     def first_hop(kind, group):
@@ -183,19 +179,25 @@
 
     LAST = len(GROUPS) - 1
 
-    def lane_hop(kind, number, source, target, peer, lanes):
+    def lane_hop(kind, out_sem, number, source, target, peer, lanes):
         lo, hi = GROUPS[LAST]
         return remote(
             source.at[kind, lo:hi, :, lanes], target.at[kind, lo:hi, :, lanes],
-            rs_s.at[kind, number, LAST], rs_r.at[kind, number, LAST], peer,
+            rs_s.at[out_sem], rs_r.at[kind, 4 * LAST + number], peer,
         )
 
-    def straight(kind, high):
-        lanes = slice(mid, cols) if high else slice(0, mid)
-        far = hop(kind, LAST, 3, s2_m, r2_m, to_far) if high else hop(kind, LAST, 2, s2_p, r2_p, to_far)
+    PIECES = ((0, BLOCK), (BLOCK, mid), (mid, cols))
+
+    def straight(kind, piece):
+        lo, hi = PIECES[piece]
+        lanes, number = slice(lo, hi), 3 * piece
+        if lo < mid:
+            far = lane_hop(kind, 2, number + 2, s2_p, r2_p, to_far, lanes)
+        else:
+            far = lane_hop(kind, 3, number + 2, s2_m, r2_m, to_far, slice(lo - mid, hi - mid))
         return [
-            lane_hop(kind, 4 if high else 0, sb_p, rb_p, to_right, lanes),
-            lane_hop(kind, 5 if high else 1, sb_m, rb_m, to_left, lanes),
+            lane_hop(kind, 0, number, sb_p, rb_p, to_right, lanes),
+            lane_hop(kind, 1, number + 1, sb_m, rb_m, to_left, lanes),
             far,
         ]
 
@@ -218,21 +220,20 @@
             put(sb_m, kind, LAST, lanes, parts[3].astype(BF))
             return carry
 
-        lax.fori_loop(0, mid // BLOCK, low, 0)
-        if not hold:
-            for copy in straight(kind, False):
-                copy.start()
-        lax.fori_loop(0, mid // BLOCK, high, 0)
-        if not hold:
-            for copy in straight(kind, True):
-                copy.start()
-
-    def reduced(kind, high):
-        for group in range(LAST):
-            second_hop(kind, group)[1 if high else 0].wait_recv()
-        for copy in straight(kind, high):
+        for piece, (body, lo, hi) in enumerate(((low, 0, 1), (low, 1, 2), (high, 0, mid // BLOCK))):
+            lax.fori_loop(lo, hi, body, 0)
+            if not hold:
+                for copy in straight(kind, piece):
+                    copy.start()
+
+    def reduced(kind, piece):
+        lo, hi = PIECES[piece]
+        if piece != 1:
+            for group in range(LAST):
+                second_hop(kind, group)[0 if lo < mid else 1].wait_recv()
+        for copy in straight(kind, piece):
             copy.wait_recv()
-        lanes, ref = (slice(mid, cols), rb_m) if high else (slice(0, mid), rb_p)
+        lanes, ref = slice(lo, hi), rb_p if lo < mid else rb_m
         put(own, kind, LAST, lanes, get(own, kind, LAST, lanes) + get(ref, kind, LAST, lanes).astype(F32))
 
     def probe_signs():
@@ -302,51 +303,54 @@
     relay(ERR, 4)
     partial_last(ERR)
     partial(TAN, 4, hold=True)
-    reduced(ERR, False)
+    reduced(ERR, 0)
 
     def own_block(kind, c):
         area = et.at[kind, c, col]
         return [
-            remote(area, area, ag_s.at[kind, 0, c], ag_r.at[kind, 0, c], to_right),
-            remote(area, area, ag_s.at[kind, 1, c], ag_r.at[kind, 1, c], to_left),
+            remote(area, area, ag_s.at[0], ag_r.at[kind, 0, c], to_right),
+            remote(area, area, ag_s.at[1], ag_r.at[kind, 1, c], to_left),
         ]
 
     def far_block(kind, c):
         first, second = slice(0, AVG // 2), slice(AVG // 2, AVG)
         low, high = et.at[kind, c, left, first], et.at[kind, c, right, second]
         return [
-            remote(low, low, ag_s.at[kind, 2, c], ag_r.at[kind, 2, c], to_right),
-            remote(high, high, ag_s.at[kind, 3, c], ag_r.at[kind, 3, c], to_left),
+            remote(low, low, ag_s.at[2], ag_r.at[kind, 2, c], to_right),
+            remote(high, high, ag_s.at[3], ag_r.at[kind, 3, c], to_left),
         ]
 
-    def first_block(c):
-        first, second = slice(0, AVG // 2), slice(AVG // 2, AVG)
-        low, high = et.at[ERR, c, col, first], et.at[ERR, c, col, second]
-        return own_block(ERR, c) + [
-            remote(low, low, ag_s.at[ERR, 2, c], ag_r.at[ERR, 2, c], to_far),
-            remote(high, high, ag_s.at[ERR, 3, c], ag_r.at[ERR, 3, c], to_far),
+    def first_rows(part):
+        return slice(part * AVG // 2, (part + 1) * AVG // 2)
+
+    def first_block(part):
+        area = et.at[ERR, 0, col, first_rows(part)]
+        return [
+            remote(area, area, ag_s.at[0], (fr.at[1] if part else ag_r.at[ERR, 0, 0]), to_right),
+            remote(area, area, ag_s.at[1], (fr.at[2] if part else ag_r.at[ERR, 1, 0]), to_left),
+            remote(area, area, ag_s.at[2 + part], ag_r.at[ERR, 2 + part, 0], to_far),
         ]
 
     PARTS = 2
     PART = half // PARTS
 
     def twin_block(c, p):
-        return remote(g_send.at[c, p], g_recv.at[c, p], co_s.at[p, c], co_r.at[p, c], twin)
+        return remote(g_send.at[c, p], g_recv.at[c, p], co_s.at[0], co_r.at[p, c], twin)
 
     def twin_means(c):
-        return remote(m_send.at[c], m_recv.at[c], co_s.at[PARTS, c], co_r.at[PARTS, c], twin)
+        return remote(m_send.at[c], m_recv.at[c], co_s.at[1], co_r.at[PARTS, c], twin)
 
     def z_block(c, p):
-        return remote(h_send.at[c, p], h_recv.at[c, p], zs.at[p, c], zr.at[p, c], zmate)
+        return remote(h_send.at[c, p], h_recv.at[c, p], zs.at[0], zr.at[p, c], zmate)
 
     def z_means(c):
-        return remote(n_send.at[c], n_recv.at[c], zs.at[PARTS, c], zr.at[PARTS, c], zmate)
+        return remote(n_send.at[c], n_recv.at[c], zs.at[1], zr.at[PARTS, c], zmate)
 
     def result(c, p):
         area = out.at[
             pl.ds(pl.multiple_of(core * half + p * PART, PART), PART), pl.ds(pl.multiple_of(c * AVG, AVG), AVG)
         ]
-        return remote(area, area, fs.at[p, c], fr.at[p, c], twin)
+        return remote(area, area, fs, fr.at[0], twin)
 
     units = own.shape[1]
     tokens = units * SUB
@@ -391,38 +395,41 @@
         x = xg[:, :, :, pl.ds(start, PART)].reshape(4 * tokens, PART)
         return jnp.dot(block, x, preferred_element_type=F32), pl.ds(start, PART)
 
-    def contract(e, t):
+    def contract(e, *tangents):
         blocks = [] if e is None else [whole(ERR, e)]
-        blocks += [] if t is None else [whole(TAN, t)]
+        blocks += [whole(TAN, t) for t in tangents]
         both = jnp.concatenate(blocks, axis=0)
-
-        def means(sums, lanes, ref, p):
-            signs = pl.ds(pl.multiple_of(t * AVG, AVG), AVG)
+        before = len(blocks) - len(tangents)
+
+        def means(sums, lanes, ref, k, p):
+            signs = pl.ds(pl.multiple_of(tangents[k] * AVG, AVG), AVG)
+            sums = sums[(before + k) * AVG:(before + k + 1) * AVG]
             mean = jnp.sum(sums * pt[signs, lanes].astype(F32), axis=0, keepdims=True) * curv_scale
-            for k in range(PART // 128):
-                at = p * (PART // 128) + k
-                ref[at:at + 1, :] = mean[:, k * 128:(k + 1) * 128]
+            for j in range(PART // 128):
+                at = p * (PART // 128) + j
+                ref[at:at + 1, :] = mean[:, j * 128:(j + 1) * 128]
 
         for p in range(PARTS):
             sums, lanes = product(both, 1 - core, p)
             if e is not None:
                 g_send[e, p] = (sums[:AVG] * grad_scale).astype(BF)
                 twin_block(e, p).start()
-            if t is not None:
-                means(sums[-AVG:], lanes, m_send.at[t], p)
-        if t is not None:
+            for k, t in enumerate(tangents):
+                means(sums, lanes, m_send.at[t], k, p)
+        for t in tangents:
             twin_means(t).start()
         for p in range(PARTS):
             sums, lanes = product(both, core, p)
             if e is not None:
                 g_own[p] = sums[:AVG] * grad_scale
-            if t is not None:
-                means(sums[-AVG:], lanes, m_own, p)
-
-    def reduce_means(t):
-        twin_means(t).wait_recv()
-        n_send[t] = m_own[...] + m_recv[t]
-        z_means(t).start()
+            for k in range(len(tangents)):
+                means(sums, lanes, m_own.at[k], k, p)
+
+    def reduce_means(*tangents):
+        for k, t in enumerate(tangents):
+            twin_means(t).wait_recv()
+            n_send[t] = m_own[k] + m_recv[t]
+            z_means(t).start()
 
     def reduce_twin(e):
         for p in range(PARTS):
@@ -449,69 +456,112 @@
         for p in range(PARTS):
             z_block(c, p).start()
 
+    def first_twin(part, p):
+        rows_ = first_rows(part)
+        return remote(
+            g_send.at[0, p, rows_], g_recv.at[0, p, rows_], co_s.at[0], (fr.at[3 + p] if part else co_r.at[p, 0]), twin
+        )
+
+    def first_z(part, p):
+        rows_ = first_rows(part)
+        return remote(h_send.at[0, p, rows_], h_recv.at[0, p, rows_], zs.at[0], zr.at[p, 0], zmate)
+
+    def first_contract(part):
+        for copy in first_block(part):
+            copy.wait_recv()
+        rows_ = first_rows(part)
+        errors = jnp.concatenate([et[ERR, 0, k, rows_] for k in range(4)], axis=1)
+        for p in range(PARTS):
+            g_send[0, p, rows_] = (product(errors, 1 - core, p)[0] * grad_scale).astype(BF)
+            first_twin(part, p).start()
+        for p in range(PARTS):
+            g_own[p, rows_] = product(errors, core, p)[0] * grad_scale
+
+    def first_reduce(part):
+        rows_ = first_rows(part)
+        for p in range(PARTS):
+            first_twin(part, p).wait_recv()
+            h_send[0, p, rows_] = (g_own[p, rows_] + g_recv[0, p, rows_].astype(F32)).astype(BF)
+            first_z(part, p).start()
+
     share(ERR, 0)
-    for copy in first_block(0):
-        copy.start()
+    for part in range(2):
+        for copy in first_block(part):
+            copy.start()
     send_share(ERR, 1)
+    reduced(ERR, 1)
     send_share(ERR, 2)
     for copy in first_hop(TAN, 3):
         copy.start()
     partial_last(TAN, hold=True)
-    for copy in own_block(ERR, 0):
-        copy.wait_recv()
-    contract(0, None)
+    first_contract(0)
+    first_reduce(0)
+    first_contract(1)
     far_share(ERR, 1)
-    send_share(ERR, 3)
-    reduce_twin(0)
-    z_start(0)
     for copy in first_hop(TAN, 4):
         copy.start()
+    first_reduce(1)
+    send_share(ERR, 3)
     relay(TAN, 3)
 
-    BACK, LAG = 5, 8
+    BACK, LAG, PAIRED = 5, 9, nc // 2
 
     def main(t, carry):
-        def when(lag):
-            return pl.when((t >= lag) & (t < nc + lag))
-
         @pl.when(t + 1 < nc)
         def _():
             far_share(ERR, t + 1)
 
-        @when(BACK - 1)
+        @pl.when((t >= BACK - 1) & (t < BACK - 1 + PAIRED))
         def _():
             far_share(TAN, t - (BACK - 1))
 
+        @pl.when((t == PAIRED + 4) | (t == PAIRED + 5))
+        def _():
+            first = PAIRED + 2 * (t - PAIRED - 4)
+            far_share(TAN, first)
+            far_share(TAN, first + 1)
+
         @pl.when(t == 1)
         def _():
-            for copy in straight(TAN, False) + straight(TAN, True):
-                copy.start()
-            reduced(ERR, True)
+            for piece in range(len(PIECES)):
+                for copy in straight(TAN, piece):
+                    copy.start()
+            reduced(ERR, 2)
 
         @pl.when(t + 3 < nc)
         def _():
             send_share(ERR, t + 3)
 
-        @pl.when((t >= 3) & (t < nc + 2))
+        @pl.when((t >= 3) & (t < PAIRED + 2))
         def _():
             send_share(TAN, t - 2)
 
+        @pl.when((t == PAIRED + 2) | (t == PAIRED + 3))
+        def _():
+            first = PAIRED + 2 * (t - PAIRED - 2)
+            send_share(TAN, first)
+            send_share(TAN, first + 1)
+
         @pl.when(t < BACK)
         def _():
-            contract(t, None)
+            contract(t)
 
         @pl.when((t >= BACK) & (t < nc))
         def _():
             contract(t, t - BACK)
-
-        @pl.when((t >= nc) & (t < nc + BACK))
-        def _():
-            contract(None, t - BACK)
-
-        @when(BACK)
-        def _():
             reduce_means(t - BACK)
 
+        @pl.when(t == nc)
+        def _():
+            contract(None, nc - BACK)
+            reduce_means(nc - BACK)
+
+        @pl.when((t == nc + 1) | (t == nc + 2))
+        def _():
+            first = PAIRED + 2 * (t - nc - 1)
+            contract(None, first, first + 1)
+            reduce_means(first, first + 1)
+
         @pl.when(t < nc)
         def _():
             reduce_twin(t)
@@ -530,11 +580,11 @@
 
         @pl.when(t == 2)
         def _():
-            reduced(TAN, False)
-            reduced(TAN, True)
+            for piece in range(len(PIECES)):
+                reduced(TAN, piece)
             send_share(TAN, 0)
 
-        @when(LAG)
+        @pl.when(t >= LAG)
         def _():
             divide(t - LAG)
 
@@ -542,28 +592,20 @@
 
     lax.fori_loop(1, nc + LAG, main, 0)
 
-    for copy in sent:
-        copy.wait_send()
-    for kind in (ERR, TAN):
-        for group in range(LAST):
-            for copy in first_hop(kind, group) + second_hop(kind, group):
-                copy.wait_send()
-        for copy in straight(kind, False) + straight(kind, True):
-            copy.wait_send()
-
-    def drain(c, carry):
-        for kind in (ERR, TAN):
-            for copy in own_block(kind, c) + far_block(kind, c):
-                copy.wait_send()
-        twin_means(c).wait_send()
-        z_means(c).wait_send()
-        for p in range(PARTS):
-            twin_block(c, p).wait_send()
-            z_block(c, p).wait_send()
-            result(c, p).wait()
-        return carry
-
-    lax.fori_loop(0, nc, drain, 0)
+    def left_for_good(area, semaphore):
+        remote(area, area, semaphore, fr.at[0], twin).wait_send()
+
+    left_for_good(xg.at[:, 0:14], xs)
+    for k, ref in enumerate((sb_p, sb_m, s2_p, s2_m)):
+        left_for_good(ref, rs_s.at[k])
+    for k in range(2):
+        left_for_good(et.at[:, :, 0], ag_s.at[k])
+        left_for_good(et.at[:, :, 0, 0:AVG // 2], ag_s.at[2 + k])
+    for k, (block, means) in enumerate(((g_send, m_send), (h_send, n_send))):
+        left_for_good(block, (co_s, zs)[k].at[0])
+        left_for_good(means, (co_s, zs)[k].at[1])
+    area = out.at[0:half]
+    remote(area, area, fs, fr.at[0], twin).wait()
 
 
 def write_out(step, out, sems):
@@ -613,7 +655,7 @@
             vmem((2, 16, SUB, cols // 2), BF),
             vmem((2, nc, 4, AVG, 256), BF),
             vmem((2, AVG, half // 2), F32),
-            vmem((8, 128), F32),
+            vmem((2, 8, 128), F32),
             vmem((nc, 2, AVG, half // 2), BF),
             vmem((nc, 8, 128), F32),
             vmem((nc, 2, AVG, half // 2), BF),
@@ -623,18 +665,18 @@
             vmem((nc, 2, AVG, half // 2), BF),
             vmem((nc, 8, 128), F32),
             dma((3,)),
-            dma((15,)),
+            dma(()),
             dma((18,)),
-            dma((2, 6, 6)),
-            dma((2, 6, 6)),
+            dma((4,)),
+            dma((2, 29)),
+            dma((4,)),
             dma((2, 4, nc)),
-            dma((2, 4, nc)),
+            dma((2,)),
             dma((3, nc)),
+            dma((2,)),
             dma((3, nc)),
-            dma((3, nc)),
-            dma((3, nc)),
-            dma((2, nc)),
-            dma((2, nc)),
+            dma(()),
+            dma((5,)),
         ],
         compiler_params=pltpu.CompilerParams(
             collective_id=0, has_side_effects=True, vmem_limit_bytes=50 * 1024 * 1024

time: 108 us -> 105 us (0.972)
  Pallas kernels: 108 us -> 104 us
    pallas_call x1, Pallas kernels: 106 us -> 102 us  [shards(): pl.pallas_call(functools.partial(kernel, 1.0 / math.sqrt(total), 1.0 / to...]
where the time goes in v4:
time: 105 us
  Pallas kernels  104 us (99%)
    pallas_call x1, Pallas kernels, shards(): pl.pallas_call(functools.partial(kernel, 1.0 / math.sqrt(total), 1.0 / to...  102 us

profile of v4, /device:TPU:1, one launch (start us, length us, event | category | flops | bytes accessed | tf_op | source)
XLA Modules:
  0.0 105.0 jit_solution(5532121830520961301)
XLA Ops:
  0.7 102.2 %shard_map.46.step = bf16[2048,1024]{1,0:T(8,128)(2,1)S(1)} custom-call(s32[1,1]{1,0:T(1,128)S(6)} %copy.5.code_ref, bf16[4,2,16,2048]{3,2,1,0:T(8,128)(2,1)} %bitcast.2, bf16[2,4,2,16,1024]{4,3,2,1,0:T(8,128)(2,1)} %bitcast.3, bf16[2048,1024]{1,0:T(8,128)(2,1)} %w_hbm.1), custom_call_target="tpu_custom_call" | custom-call | tf_op jit(solution)/shard_map/pallas_call | solution.py:635
  102.8 2.0 %shard_map.47 = bf16[2048,1024]{1,0:T(8,128)(2,1)} custom-call(bf16[2048,1024]{1,0:T(8,128)(2,1)S(1)} %shard_map.46.step), custom_call_target="tpu_custom_call" | custom-call | tf_op jit(solution)/shard_map/pallas_call | solution.py:685
